TPU v7x, 32 devices: a whole 2x2x4 slice. The times are simulated.
32 devices in a mesh: groups: 2 (over x), frame: 16 (over z, y, core).
Axes of the slice: x: 2, y: 2, z: 4, core: 2. Of those that a mesh axis runs over, the one named last changes fastest.
Arguments:
- query_in: bfloat16 [32, 512, 1536], P(('groups', 'frame')), parts along dimension 0, may hold values from -200 to 200, as said below
- keys_in: bfloat16 [32, 512, 1536], P(('groups', 'frame')), parts along dimension 0, may hold values from -7 to 7, as said below
- values_in: bfloat16 [32, 512, 1536], P(('groups', 'frame')), parts along dimension 0, may hold values from -6 to 6
- far_picks: int32 [32, 6], P('groups'), parts along dimension 0, may hold values from 0 to 3
- win_rows: int32 [32], P(('groups', 'frame')), parts along dimension 0, may hold values from 1 to 15, as said below
Outputs:
- attended: bfloat16 [32, 512, 1536], P(('groups', 'frame')), parts along dimension 0
There are 2 independent parts, one for each index of `groups`. A program takes and returns all parts, laid end to end along the dimension named above; each array names one. Nothing has to cross between parts.
Inputs may be any that keep to these rules, and one draw needn't show every extreme that they name: `query_in`: entries of the queries lie within this range. `keys_in`: entries of the keys lie within this range. `win_rows`: every draw has a frame with window 1 and a frame with window 16 - 1.
All inputs are finite; a program needn't handle non-finite values.
Results may differ from a plain program's by a relative error of at most 0.0032.
Values may be sent and summed in bfloat16 or wider, within the bound.
No kernel may reach another device: no remote copies, remote signals or barrier semaphores. Data moves between devices by JAX's collectives and lax.ppermute only.
A program may use at most 128 MiB of HBM per device.

v0:
```python
import functools
import math

import jax
import jax.numpy as jnp
from jax import lax
from jax.experimental import pallas as pl
from jax.experimental.pallas import tpu as pltpu
from jax.sharding import PartitionSpec as P

HD = 128
COLS = 32
SUB = 128
NREACH = 3
MASKED = -1e30
BASE2 = math.log2(math.e) / math.sqrt(HD)
ONES = 16


def offsets_for(frames):
    spacing = [frames // 2 ** (NREACH - level_index) for level_index in range(NREACH)]
    return [-stride for stride in spacing] + [stride for stride in spacing]


def moved(value, steps):
    count = lax.axis_size("frame")
    pairs = [(f, f + step) for step, who in steps for f in range(count) if who(f)]
    pairs = [(source, target) for source, target in pairs if 0 <= target < count]
    return lax.ppermute(value, "frame", pairs)


def anyone(frame):
    return True


def is_even(frame):
    return frame % 2 == 0


def is_odd(frame):
    return frame % 2 == 1


def gather_kernel(readers, frames, picks_ref, keys_ref, values_ref, *refs):
    outs, sems = refs[: len(readers)], refs[len(readers)]
    width = keys_ref.shape[1]
    position = lax.axis_index("frame")
    copies = []
    for slot, (reader_of, out) in enumerate(zip(readers, outs)):
        reader, column = reader_of(position)
        pick = picks_ref[jnp.clip(reader, 0, frames - 1), column]
        rows = pl.ds(pl.multiple_of(pick * SUB, SUB), SUB)
        for half, source in enumerate((keys_ref, values_ref)):
            target = out.at[:, pl.ds(half * width, width)]
            copies.append(
                pltpu.make_async_copy(source.at[rows, :], target, sems.at[2 * slot + half])
            )
    for copy in copies:
        copy.start()
    for copy in copies:
        copy.wait()


def gather(picks, keys, values, readers, frames):
    width = keys.shape[1]
    shape = (SUB, 2 * width)
    return pl.pallas_call(
        functools.partial(gather_kernel, readers, frames),
        out_shape=[jax.ShapeDtypeStruct(shape, keys.dtype) for _ in readers],
        in_specs=[
            pl.BlockSpec(memory_space=pltpu.SMEM),
            pl.BlockSpec(memory_space=pl.ANY),
            pl.BlockSpec(memory_space=pl.ANY),
        ],
        out_specs=[pl.BlockSpec(memory_space=pltpu.VMEM) for _ in readers],
        scratch_shapes=[pltpu.SemaphoreType.DMA((2 * len(readers),))],
        compiler_params=pltpu.CompilerParams(vmem_limit_bytes=60 << 20),
        cost_estimate=pl.CostEstimate(
            flops=0, bytes_accessed=8 * SUB * width * len(readers), transcendentals=0
        ),
    )(picks, keys, values)


def attend_kernel(kinds, together, first, last, window_ref, q_ref, *refs):
    count = len(kinds)
    sources = [(refs[2 * i], refs[2 * i + 1]) for i in range(count)]
    refs = refs[2 * count :]
    if not first:
        acc_in, stat_in = refs[:2]
        refs = refs[2:]
    if last:
        out_ref, bias_ref, class_ref, turned_ref = refs
    else:
        acc_out, stat_out, bias_ref, class_ref, turned_ref = refs
    tokens = q_ref.shape[0]
    sizes = [key_ref.shape[0] for key_ref, _ in sources]

    @pl.when(pl.program_id(0) == 0)
    def _():
        position = lax.axis_index("frame")
        row = lax.broadcasted_iota(jnp.int32, (tokens, HD), 0) // COLS
        lane = lax.broadcasted_iota(jnp.int32, (tokens, HD), 1)
        bias = jnp.zeros((tokens, HD), jnp.float32)
        base, start = 0, 0
        for (windowed, there), size in zip(kinds, sizes):
            there = there(position)
            if windowed:
                wide = size // COLS
                here = jnp.abs(row - (lane - base)) <= jnp.where(there, window_ref[0], -1)
                hot = row[:size] == lane[:size] - base
            else:
                wide = 1
                here = lane * 0 + jnp.where(there, 1, 0) > 0
                hot = lane[:size] == base
            mine = (lane >= base) & (lane < base + wide)
            bias = jnp.where(mine & ~here, MASKED, bias)
            class_ref[pl.ds(start, size), :] = jnp.where(hot, 1.0, 0.0).astype(jnp.bfloat16)
            base, start = base + wide, start + size
        bias_ref[...] = bias.astype(jnp.bfloat16)
        turned_ref[:, pl.ds(HD, ONES), :] = jnp.ones((together, ONES, sum(sizes)), jnp.bfloat16)

    def column(head):
        return pl.ds(head * HD, HD)

    def scores_of(head):
        keys = jnp.concatenate([key_ref[:, column(head)] for key_ref, _ in sources], axis=0)
        keys = jnp.concatenate([keys, class_ref[...]], axis=1)
        query = jnp.concatenate([q_ref[:, column(head)], bias_ref[...]], axis=1)
        scores = lax.dot_general(
            keys, query, (((1,), (1,)), ((), ())), preferred_element_type=jnp.float32
        )
        return scores, jnp.max(scores, axis=0, keepdims=True)

    for head in range(together):
        start = 0
        for (_, value_ref), size in zip(sources, sizes):
            turned_ref[head, pl.ds(0, HD), pl.ds(start, size)] = value_ref[:, column(head)].T
            start += size
    upcoming = scores_of(0)
    for head in range(together):
        scores, peak = upcoming
        if head + 1 < together:
            upcoming = scores_of(head + 1)
        if not first:
            before = stat_in[8 * head : 8 * head + 1, :]
            peak = jnp.maximum(peak, before)
        weights = jnp.exp2((scores - peak) * BASE2).astype(jnp.bfloat16)
        total = jnp.dot(turned_ref[head], weights, preferred_element_type=jnp.float32)
        acc, norm = total[:HD, :], total[HD : HD + 1, :]
        if not first:
            scale = jnp.exp2((before - peak) * BASE2)
            acc = acc + acc_in[column(head), :] * scale
            norm = norm + stat_in[8 * head + 1 : 8 * head + 2, :] * scale
        if last:
            out_ref[:, column(head)] = (acc / norm).T.astype(out_ref.dtype)
        else:
            acc_out[column(head), :] = acc
            stat_out[8 * head : 8 * head + 1, :] = peak
            stat_out[8 * head + 1 : 8 * head + 2, :] = norm


def attend(window, query, sources, state, last):
    tokens, width = query.shape
    heads = width // HD
    together = next(n for n in (3, 2, 1) if heads % n == 0)
    kinds = tuple(source[4:] for source in sources)

    def columns(rows, base):
        return pl.BlockSpec((rows, HD * together), lambda h, window: (0, base // together + h))

    specs, operands = [columns(tokens, 0)], [query]
    keys_count = 0
    for key, key_base, value, value_base, _, _ in sources:
        specs += [columns(key.shape[0], key_base), columns(key.shape[0], value_base)]
        operands += [key, value]
        keys_count += key.shape[0]
    state_specs = [
        pl.BlockSpec((HD * together, tokens), lambda h, window: (h, 0)),
        pl.BlockSpec((8 * together, tokens), lambda h, window: (h, 0)),
    ]
    moved_bytes = 2 * (tokens + 2 * keys_count) * width
    if state is not None:
        specs += state_specs
        operands += list(state)
        moved_bytes += 4 * tokens * width
    if last:
        out_shape = jax.ShapeDtypeStruct((tokens, width), jnp.bfloat16)
        out_specs = columns(tokens, 0)
    else:
        out_shape = [
            jax.ShapeDtypeStruct((width, tokens), jnp.float32),
            jax.ShapeDtypeStruct((8 * heads, tokens), jnp.float32),
        ]
        out_specs = state_specs
    return pl.pallas_call(
        functools.partial(attend_kernel, kinds, together, state is None, last),
        out_shape=out_shape,
        grid_spec=pltpu.PrefetchScalarGridSpec(
            num_scalar_prefetch=1,
            grid=(heads // together,),
            in_specs=specs,
            out_specs=out_specs,
            scratch_shapes=[
                pltpu.VMEM((tokens, HD), jnp.bfloat16),
                pltpu.VMEM((keys_count, HD), jnp.bfloat16),
                pltpu.VMEM((together, HD + ONES, keys_count), jnp.bfloat16),
            ],
        ),
        compiler_params=pltpu.CompilerParams(vmem_limit_bytes=60 << 20),
        cost_estimate=pl.CostEstimate(
            flops=4 * tokens * keys_count * width,
            bytes_accessed=moved_bytes + 2 * tokens * width,
            transcendentals=tokens * keys_count * heads,
        ),
    )(window, *operands)


def body(query_in, keys_in, values_in, far_picks, win_rows):
    frames = lax.axis_size("frame")
    query, keys, values = query_in[0], keys_in[0], values_in[0]
    heads = query.shape[1] // HD
    offsets = offsets_for(frames)
    shared = frames % 2 == 0 and 2 in offsets

    def beyond_of(position):
        return position + 2 * (position % 2) - 1

    def there(frame):
        return (frame >= 0) & (frame < frames)

    outward = [(1, is_odd), (-1, is_even)]
    inward = [(1, is_even), (-1, is_odd)]
    beyond_keys = moved(keys, outward)
    beyond_values = moved(values, outward)
    beyond = [beyond_keys, beyond_values]

    far = []
    for column in sorted(range(len(offsets)), key=lambda c: -abs(offsets[c])):
        offset = offsets[column]
        if shared and abs(offset) == 2:
            continue
        if 2 * abs(offset) == frames:
            if offset > 0:
                continue
            back, ahead = column, offsets.index(-offset)
            half = -offset

            def across(position, half=half, back=back, ahead=ahead):
                low = position < half
                return position + jnp.where(low, half, -half), jnp.where(low, back, ahead)

            steps = [(half, lambda f, half=half: f < half), (-half, lambda f, half=half: f >= half)]
            far.append((steps, across, lambda position: position >= 0))
            continue
        far.append(
            (
                [(-offset, anyone)],
                lambda position, offset=offset, column=column: (position - offset, column),
                lambda position, offset=offset: there(position + offset),
            )
        )
    if shared:
        back, ahead = offsets.index(-2), offsets.index(2)

        def two_on(position):
            odd = position % 2
            return position + 2 - 4 * odd, jnp.where(odd == 0, back, ahead)

        def two_back(position):
            return there(position - 2 + 4 * (position % 2))

        def partner(position):
            odd = position % 2
            return position + 1 - 2 * odd, jnp.where(odd == 0, back, ahead)

        far.append(([(2, is_even), (-2, is_odd)], two_on, two_back))
    blocks = gather(far_picks, keys, values, [reader for _, reader, _ in far], frames)
    arrived = []
    for block, (steps, _, _) in zip(blocks, far):
        arrived.append(moved(block, steps))
    mate_keys = moved(keys, inward)
    mate_values = moved(values, inward)

    def always(position):
        return position >= 0

    def near_there(position):
        return there(beyond_of(position))

    own = [(keys, 0, values, 0, True, always), (mate_keys, 0, mate_values, 0, True, always)]
    state = attend(win_rows, query, own, None, False)
    nearby = [(beyond[0], 0, beyond[1], 0, True, near_there)]
    if shared:
        (handed,) = gather(far_picks, *beyond, [partner], frames)
        handed = moved(handed, inward)
        nearby.append(
            (handed, 0, handed, heads, False, lambda p: there(p + 2 - 4 * (p % 2)))
        )
    state = attend(win_rows, query, nearby, state, False)
    distant = [
        (block, 0, block, heads, False, there) for block, (_, _, there) in zip(arrived, far)
    ]
    return attend(win_rows, query, distant, state, True)[None]


def solution(mesh):
    in_specs = (
        P(("groups", "frame"), None, None),
        P(("groups", "frame"), None, None),
        P(("groups", "frame"), None, None),
        P("groups", None),
        P(("groups", "frame")),
    )
    out_specs = P(("groups", "frame"), None, None)

    return jax.shard_map(body, mesh=mesh, in_specs=in_specs, out_specs=out_specs, check_vma=False)
```

profile of v0, /device:TPU:18, one launch (start us, length us, event | category | flops | bytes accessed | tf_op | source)
XLA Modules:
  0.0 153.5 jit_solution(4856960130525844653)
XLA Ops:
  0.0 2.7 %collective-permute-start.4 = (bf16[512,1536]{1,0:T(8,128)(2,1)}, bf16[512,1536]{1,0:T(8,128)(2,1)S(1)}, u32[]{:S(2)}, u32[]{:S(2)}) collective-permute-start(bf16[512,1536]{1,0:T(8,128)(2,1)} %bitcast.7), channel_id=1, source_target_pairs={{1,2},{3,4},{5,6},{7,8},{9,10},{11,12},{13,14},{2,1},{4,3},{6,5},{... | collective-permute-start | bytes 4718600 | tf_op jit(solution)/shard_map/ppermute | solution.py:29
  2.8 3.7 %collective-permute-start.5 = (bf16[512,1536]{1,0:T(8,128)(2,1)}, bf16[512,1536]{1,0:T(8,128)(2,1)S(1)}, u32[]{:S(2)}, u32[]{:S(2)}) collective-permute-start(bf16[512,1536]{1,0:T(8,128)(2,1)} %bitcast.11), channel_id=1, source_target_pairs={{1,2},{3,4},{5,6},{7,8},{9,10},{11,12},{13,14},{2,1},{4,3},{6,5},{... | collective-permute-start | bytes 4718600 | tf_op jit(solution)/shard_map/ppermute | solution.py:29
  6.5 0.1 collective-permute-start.7
  6.6 0.5 collective-permute-start.8
  7.0 1.4 copy.6.picks_ref
  8.4 14.5 %collective-permute-done.4.keys_ref.refs_0_ = bf16[512,1536]{1,0:T(8,128)(2,1)S(1)} collective-permute-done((bf16[512,1536]{1,0:T(8,128)(2,1)}, bf16[512,1536]{1,0:T(8,128)(2,1)S(1)}, u32[]{:S(2)}, u32[]{:S(2)}) %collective-permute-start.4) | collective-permute-done | bytes 1572896 | tf_op jit(solution)/shard_map/ppermute | solution.py:29
  22.9 0.0 copy-start
  22.9 16.9 %collective-permute-done.5.values_ref.refs_1_ = bf16[512,1536]{1,0:T(8,128)(2,1)S(1)} collective-permute-done((bf16[512,1536]{1,0:T(8,128)(2,1)}, bf16[512,1536]{1,0:T(8,128)(2,1)S(1)}, u32[]{:S(2)}, u32[]{:S(2)}) %collective-permute-start.5) | collective-permute-done | bytes 1572896 | tf_op jit(solution)/shard_map/ppermute | solution.py:29
  39.8 0.0 copy-done
  39.8 0.0 copy-start.1
  39.8 1.2 copy-done.1
  41.0 2.8 %shard_map.56 = bf16[128,3072]{1,0:T(8,128)(2,1)} custom-call(s32[16,6]{1,0:T(8,128)} %copy.6.picks_ref, bf16[512,1536]{1,0:T(8,128)(2,1)} %copy-done, bf16[512,1536]{1,0:T(8,128)(2,1)} %copy-done.1), custom_call_target="tpu_custom_call" | custom-call | bytes 1572864 | tf_op jit(solution)/shard_map/pallas_call | solution.py:67
  43.8 32.7 %collective-permute-start.6 = (bf16[128,3072]{1,0:T(8,128)(2,1)}, bf16[128,3072]{1,0:T(8,128)(2,1)S(1)}, u32[]{:S(2)}, u32[]{:S(2)}) collective-permute-start(bf16[128,3072]{1,0:T(8,128)(2,1)} %shard_map.56), channel_id=1, source_target_pairs={{0,1},{2,3},{4,5},{6,7},{8,9},{10,11},{12,13},{14,15},{1,0},{3,2},... | collective-permute-start | bytes 2359304 | tf_op jit(solution)/shard_map/ppermute | solution.py:29
  76.4 4.5 %shard_map.55 = (bf16[128,3072]{1,0:T(8,128)(2,1)}, bf16[128,3072]{1,0:T(8,128)(2,1)}, bf16[128,3072]{1,0:T(8,128)(2,1)}, bf16[128,3072]{1,0:T(8,128)(2,1)}) custom-call(s32[16,6]{1,0:T(8,128)} %copy.6.picks_ref, bf16[512,1536]{1,0:T(8,128)(2,1)} %bitcast.9, bf16[512,1536]{1,0:T(8,128)(2,1)} %bitcast.13), custom_call_target="tpu_custom_call" | custom-call | bytes 6291456 | tf_op jit(solution)/shard_map/pallas_call | solution.py:67
  80.9 0.1 collective-permute-start
  81.0 3.8 %collective-permute-start.1 = (bf16[128,3072]{1,0:T(8,128)(2,1)}, bf16[128,3072]{1,0:T(8,128)(2,1)S(1)}, u32[]{:S(2)}, u32[]{:S(2)}) collective-permute-start(bf16[128,3072]{1,0:T(8,128)(2,1)} %get-tuple-element.14), channel_id=1, source_target_pairs={{0,4},{1,5},{2,6},{3,7},{4,8},{5,9},{6,10},{7,11},{8,12},{9,13},{1... | collective-permute-start | bytes 2359304 | tf_op jit(solution)/shard_map/ppermute | solution.py:29
  84.8 0.0 collective-permute-done.7.refs_2_
  84.8 3.0 %collective-permute-start.2 = (bf16[128,3072]{1,0:T(8,128)(2,1)}, bf16[128,3072]{1,0:T(8,128)(2,1)S(1)}, u32[]{:S(2)}, u32[]{:S(2)}) collective-permute-start(bf16[128,3072]{1,0:T(8,128)(2,1)} %get-tuple-element.15), channel_id=1, source_target_pairs={{4,0},{5,1},{6,2},{7,3},{8,4},{9,5},{10,6},{11,7},{12,8},{13,9},{1... | collective-permute-start | bytes 2359304 | tf_op jit(solution)/shard_map/ppermute | solution.py:29
  87.9 0.0 collective-permute-done.8.refs_3_
  87.9 2.9 %collective-permute-start.3 = (bf16[128,3072]{1,0:T(8,128)(2,1)}, bf16[128,3072]{1,0:T(8,128)(2,1)S(1)}, u32[]{:S(2)}, u32[]{:S(2)}) collective-permute-start(bf16[128,3072]{1,0:T(8,128)(2,1)} %get-tuple-element.16), channel_id=1, source_target_pairs={{0,2},{2,4},{4,6},{6,8},{8,10},{10,12},{12,14},{3,1},{5,3},{7,5},{... | collective-permute-start | bytes 2359304 | tf_op jit(solution)/shard_map/ppermute | solution.py:29
  91.4 12.2 %shard_map.57 = (f32[1536,512]{1,0:T(8,128)}, f32[96,512]{1,0:T(8,128)}) custom-call(s32[1]{0:T(128)S(6)} %copy.8.window_ref, bf16[512,1536]{1,0:T(8,128)(2,1)} %bitcast.4, bf16[512,1536]{1,0:T(8,128)(2,1)} %bitcast.10, bf16[512,1536]{1,0:T(8,128)(2,1)} %bitcast.14, bf16[512,1536]{1,0:T(8,128)(2,1)} %collective-permute-done.7.refs_2_, ...), custom_call_target="tpu_custom_call" | custom-call | flops 3221225472 | bytes 9437184 | tf_op jit(solution)/shard_map/pallas_call | solution.py:195
  103.6 0.0 collective-permute-done.6.refs_2_.refs_3_
  103.6 0.0 copy-start.5
  103.6 0.9 copy-done.5
  104.4 9.7 %shard_map.58 = (f32[1536,512]{1,0:T(8,128)}, f32[96,512]{1,0:T(8,128)}) custom-call(s32[1]{0:T(128)S(6)} %copy.8.window_ref, bf16[512,1536]{1,0:T(8,128)(2,1)} %bitcast.5, bf16[512,1536]{1,0:T(8,128)(2,1)} %copy-done, bf16[512,1536]{1,0:T(8,128)(2,1)} %copy-done.1, bf16[128,3072]{1,0:T(8,128)(2,1)} %copy-done.5, bf16[128,3072]{1,0:T(8,128)(2,1)} %copy-done.5, ...), custom_call_target="tpu_custom_call" | custom-call | flops 2013265920 | bytes 10223616 | tf_op jit(solution)/shard_map/pallas_call | solution.py:195
  114.1 2.0 %collective-permute-done.refs_0_.refs_1_ = bf16[128,3072]{1,0:T(8,128)(2,1)S(1)} collective-permute-done((bf16[128,3072]{1,0:T(8,128)(2,1)}, bf16[128,3072]{1,0:T(8,128)(2,1)S(1)}, u32[]{:S(2)}, u32[]{:S(2)}) %collective-permute-start) | collective-permute-done | bytes 786464 | tf_op jit(solution)/shard_map/ppermute | solution.py:29
  116.1 0.0 copy-start.2
  116.1 19.3 %collective-permute-done.1.refs_2_.refs_3_ = bf16[128,3072]{1,0:T(8,128)(2,1)S(1)} collective-permute-done((bf16[128,3072]{1,0:T(8,128)(2,1)}, bf16[128,3072]{1,0:T(8,128)(2,1)S(1)}, u32[]{:S(2)}, u32[]{:S(2)}) %collective-permute-start.1) | collective-permute-done | bytes 786464 | tf_op jit(solution)/shard_map/ppermute | solution.py:29
  135.4 0.0 copy-start.3
  135.4 0.0 collective-permute-done.2.refs_4_.refs_5_
  135.4 0.0 copy-start.4
  135.4 8.2 %collective-permute-done.3.refs_6_.refs_7_ = bf16[128,3072]{1,0:T(8,128)(2,1)S(1)} collective-permute-done((bf16[128,3072]{1,0:T(8,128)(2,1)}, bf16[128,3072]{1,0:T(8,128)(2,1)S(1)}, u32[]{:S(2)}, u32[]{:S(2)}) %collective-permute-start.3) | collective-permute-done | bytes 786464 | tf_op jit(solution)/shard_map/ppermute | solution.py:29
  143.6 0.0 copy-start.6
  143.6 0.0 copy-done.2
  143.6 0.0 copy-done.3
  143.6 0.0 copy-done.4
  143.6 0.9 copy-done.6
  144.5 9.0 %shard_map.59 = bf16[512,1536]{1,0:T(8,128)(2,1)} custom-call(s32[1]{0:T(128)S(6)} %copy.8.window_ref, bf16[512,1536]{1,0:T(8,128)(2,1)} %bitcast.6, bf16[128,3072]{1,0:T(8,128)(2,1)} %copy-done.2, bf16[128,3072]{1,0:T(8,128)(2,1)} %copy-done.2, bf16[128,3072]{1,0:T(8,128)(2,1)} %copy-done.3, bf16[128,3072]{1,0:T(8,128)(2,1)} %copy-done.3, ...), custom_call_target="tpu_custom_call" | custom-call | flops 1610612736 | bytes 9437184 | tf_op jit(solution)/shard_map/pallas_call | solution.py:195
Async XLA Ops:
  0.0 22.9 %collective-permute-start.4 = (bf16[512,1536]{1,0:T(8,128)(2,1)}, bf16[512,1536]{1,0:T(8,128)(2,1)S(1)}, u32[]{:S(2)}, u32[]{:S(2)}) collective-permute-start(bf16[512,1536]{1,0:T(8,128)(2,1)} %bitcast.7), channel_id=1, source_target_pairs={{1,2},{3,4},{5,6},{7,8},{9,10},{11,12},{13,14},{2,1},{4,3},{6,5},{... | collective-permute-start | bytes 4718600 | tf_op jit(solution)/shard_map/ppermute | solution.py:29
  2.8 37.0 %collective-permute-start.5 = (bf16[512,1536]{1,0:T(8,128)(2,1)}, bf16[512,1536]{1,0:T(8,128)(2,1)S(1)}, u32[]{:S(2)}, u32[]{:S(2)}) collective-permute-start(bf16[512,1536]{1,0:T(8,128)(2,1)} %bitcast.11), channel_id=1, source_target_pairs={{1,2},{3,4},{5,6},{7,8},{9,10},{11,12},{13,14},{2,1},{4,3},{6,5},{... | collective-permute-start | bytes 4718600 | tf_op jit(solution)/shard_map/ppermute | solution.py:29
  6.5 78.3 %collective-permute-start.7 = (bf16[512,1536]{1,0:T(8,128)(2,1)}, bf16[512,1536]{1,0:T(8,128)(2,1)}, u32[]{:S(2)}, u32[]{:S(2)}) collective-permute-start(bf16[512,1536]{1,0:T(8,128)(2,1)} %bitcast.8), channel_id=1, source_target_pairs={{0,1},{2,3},{4,5},{6,7},{8,9},{10,11},{12,13},{14,15},{1,0},{3,2},... | collective-permute-start | bytes 4718600 | tf_op jit(solution)/shard_map/ppermute | solution.py:29
  6.6 81.3 %collective-permute-start.8 = (bf16[512,1536]{1,0:T(8,128)(2,1)}, bf16[512,1536]{1,0:T(8,128)(2,1)}, u32[]{:S(2)}, u32[]{:S(2)}) collective-permute-start(bf16[512,1536]{1,0:T(8,128)(2,1)} %bitcast.12), channel_id=1, source_target_pairs={{0,1},{2,3},{4,5},{6,7},{8,9},{10,11},{12,13},{14,15},{1,0},{3,2},... | collective-permute-start | bytes 4718600 | tf_op jit(solution)/shard_map/ppermute | solution.py:29
  22.9 16.9 %copy-start = (bf16[512,1536]{1,0:T(8,128)(2,1)}, bf16[512,1536]{1,0:T(8,128)(2,1)S(1)}, u32[]{:S(2)}) copy-start(bf16[512,1536]{1,0:T(8,128)(2,1)S(1)} %collective-permute-done.4.keys_ref.refs_0_) | copy-start | bytes 4718596
  39.8 1.2 copy-start.1
  43.8 59.8 %collective-permute-start.6 = (bf16[128,3072]{1,0:T(8,128)(2,1)}, bf16[128,3072]{1,0:T(8,128)(2,1)S(1)}, u32[]{:S(2)}, u32[]{:S(2)}) collective-permute-start(bf16[128,3072]{1,0:T(8,128)(2,1)} %shard_map.56), channel_id=1, source_target_pairs={{0,1},{2,3},{4,5},{6,7},{8,9},{10,11},{12,13},{14,15},{1,0},{3,2},... | collective-permute-start | bytes 2359304 | tf_op jit(solution)/shard_map/ppermute | solution.py:29
  80.9 35.2 %collective-permute-start = (bf16[128,3072]{1,0:T(8,128)(2,1)}, bf16[128,3072]{1,0:T(8,128)(2,1)S(1)}, u32[]{:S(2)}, u32[]{:S(2)}) collective-permute-start(bf16[128,3072]{1,0:T(8,128)(2,1)} %get-tuple-element.13), channel_id=1, source_target_pairs={{0,8},{1,9},{2,10},{3,11},{4,12},{5,13},{6,14},{7,15},{8,0},{9,1},... | collective-permute-start | bytes 2359304 | tf_op jit(solution)/shard_map/ppermute | solution.py:29
  81.0 54.4 %collective-permute-start.1 = (bf16[128,3072]{1,0:T(8,128)(2,1)}, bf16[128,3072]{1,0:T(8,128)(2,1)S(1)}, u32[]{:S(2)}, u32[]{:S(2)}) collective-permute-start(bf16[128,3072]{1,0:T(8,128)(2,1)} %get-tuple-element.14), channel_id=1, source_target_pairs={{0,4},{1,5},{2,6},{3,7},{4,8},{5,9},{6,10},{7,11},{8,12},{9,13},{1... | collective-permute-start | bytes 2359304 | tf_op jit(solution)/shard_map/ppermute | solution.py:29
  84.8 50.6 %collective-permute-start.2 = (bf16[128,3072]{1,0:T(8,128)(2,1)}, bf16[128,3072]{1,0:T(8,128)(2,1)S(1)}, u32[]{:S(2)}, u32[]{:S(2)}) collective-permute-start(bf16[128,3072]{1,0:T(8,128)(2,1)} %get-tuple-element.15), channel_id=1, source_target_pairs={{4,0},{5,1},{6,2},{7,3},{8,4},{9,5},{10,6},{11,7},{12,8},{13,9},{1... | collective-permute-start | bytes 2359304 | tf_op jit(solution)/shard_map/ppermute | solution.py:29
  87.9 55.7 %collective-permute-start.3 = (bf16[128,3072]{1,0:T(8,128)(2,1)}, bf16[128,3072]{1,0:T(8,128)(2,1)S(1)}, u32[]{:S(2)}, u32[]{:S(2)}) collective-permute-start(bf16[128,3072]{1,0:T(8,128)(2,1)} %get-tuple-element.16), channel_id=1, source_target_pairs={{0,2},{2,4},{4,6},{6,8},{8,10},{10,12},{12,14},{3,1},{5,3},{7,5},{... | collective-permute-start | bytes 2359304 | tf_op jit(solution)/shard_map/ppermute | solution.py:29
  103.6 0.9 copy-start.5
  116.1 27.5 %copy-start.2 = (bf16[128,3072]{1,0:T(8,128)(2,1)}, bf16[128,3072]{1,0:T(8,128)(2,1)S(1)}, u32[]{:S(2)}) copy-start(bf16[128,3072]{1,0:T(8,128)(2,1)S(1)} %collective-permute-done.refs_0_.refs_1_) | copy-start | bytes 2359300
  135.4 8.2 %copy-start.3 = (bf16[128,3072]{1,0:T(8,128)(2,1)}, bf16[128,3072]{1,0:T(8,128)(2,1)S(1)}, u32[]{:S(2)}) copy-start(bf16[128,3072]{1,0:T(8,128)(2,1)S(1)} %collective-permute-done.1.refs_2_.refs_3_) | copy-start | bytes 2359300
  135.4 8.2 %copy-start.4 = (bf16[128,3072]{1,0:T(8,128)(2,1)}, bf16[128,3072]{1,0:T(8,128)(2,1)S(1)}, u32[]{:S(2)}) copy-start(bf16[128,3072]{1,0:T(8,128)(2,1)S(1)} %collective-permute-done.2.refs_4_.refs_5_) | copy-start | bytes 2359300
  143.6 0.9 copy-start.6
where the time goes:
time: 154 us
  waiting for transfers between devices  60.9 us (40%)
  starting transfers between devices  49.5 us (32%)
  Pallas kernels  38.2 us (25%)
  local copies, waits for them, and re-layouts  4.28 us (3%)
    ppermute x9, waiting for transfers between devices, moved(): return lax.ppermute(value, 'frame', pairs)  60.9 us
    ppermute x9, starting transfers between devices, moved(): return lax.ppermute(value, 'frame', pairs)  49.5 us
    pallas_call x3, Pallas kernels, attend(): pl.pallas_call(functools.partial(attend_kernel, kinds, together, state is...  30.9 us
    pallas_call x2, Pallas kernels, gather(): pl.pallas_call(functools.partial(gather_kernel, readers, frames), out_sha...  7.27 us
    unnamed x15, local copies, waits for them, and re-layouts  4.28 us
  transfers between devices with their start and end apart: 9, of which 5 were waited for; matrix products, arithmetic and copies ran while one was open for 1% of the time, Pallas kernels for 19%

commit v1 on v0

--- a/solution.py
+++ b/solution.py
@@ -48,7 +48,7 @@
     copies = []
     for slot, (reader_of, out) in enumerate(zip(readers, outs)):
         reader, column = reader_of(position)
-        pick = picks_ref[jnp.clip(reader, 0, frames - 1), column]
+        pick = picks_ref[column, jnp.clip(reader, 0, frames - 1)]
         rows = pl.ds(pl.multiple_of(pick * SUB, SUB), SUB)
         for half, source in enumerate((keys_ref, values_ref)):
             target = out.at[:, pl.ds(half * width, width)]
@@ -69,16 +69,16 @@
         out_shape=[jax.ShapeDtypeStruct(shape, keys.dtype) for _ in readers],
         in_specs=[
             pl.BlockSpec(memory_space=pltpu.SMEM),
-            pl.BlockSpec(memory_space=pl.ANY),
-            pl.BlockSpec(memory_space=pl.ANY),
+            pl.BlockSpec(memory_space=pltpu.HBM),
+            pl.BlockSpec(memory_space=pltpu.HBM),
         ],
         out_specs=[pl.BlockSpec(memory_space=pltpu.VMEM) for _ in readers],
         scratch_shapes=[pltpu.SemaphoreType.DMA((2 * len(readers),))],
-        compiler_params=pltpu.CompilerParams(vmem_limit_bytes=60 << 20),
+        compiler_params=pltpu.CompilerParams(vmem_limit_bytes=67_043_328),
         cost_estimate=pl.CostEstimate(
             flops=0, bytes_accessed=8 * SUB * width * len(readers), transcendentals=0
         ),
-    )(picks, keys, values)
+    )(picks.T, keys, values)
 
 
 def attend_kernel(kinds, together, first, last, window_ref, q_ref, *refs):
@@ -206,7 +206,7 @@
                 pltpu.VMEM((together, HD + ONES, keys_count), jnp.bfloat16),
             ],
         ),
-        compiler_params=pltpu.CompilerParams(vmem_limit_bytes=60 << 20),
+        compiler_params=pltpu.CompilerParams(vmem_limit_bytes=67_043_328),
         cost_estimate=pl.CostEstimate(
             flops=4 * tokens * keys_count * width,
             bytes_accessed=moved_bytes + 2 * tokens * width,

time: 154 us -> 152 us (0.987)
  local copies, waits for them, and re-layouts: 4.28 us -> 0 us
  waiting for transfers between devices: 60.9 us -> 63.3 us
    unnamed x15 -> x0, local copies, waits for them, and re-layouts: 4.28 us -> none
    ppermute x9, waiting for transfers between devices: 60.9 us -> 63.3 us  [moved(): return lax.ppermute(value, 'frame', pairs)]
  transfers between devices with their start and end apart: 9 -> 9, of which waited for: 5 -> 5; matrix products, arithmetic and copies ran while one was open for 1% -> 0% of each run, Pallas kernels for 19% -> 19%
where the time goes in v1:
time: 152 us; the launch traced here: 151 us
  waiting for transfers between devices  63.3 us (42%)
  starting transfers between devices  49.5 us (33%)
  Pallas kernels  37.9 us (25%)
    ppermute x9, waiting for transfers between devices, moved(): return lax.ppermute(value, 'frame', pairs)  63.3 us
    ppermute x9, starting transfers between devices, moved(): return lax.ppermute(value, 'frame', pairs)  49.5 us
    pallas_call x3, Pallas kernels, attend(): pl.pallas_call(functools.partial(attend_kernel, kinds, together, state is...  30.9 us
    pallas_call x2, Pallas kernels, gather(): pl.pallas_call(functools.partial(gather_kernel, readers, frames), out_sha...  7.07 us
  transfers between devices with their start and end apart: 9, of which 5 were waited for; matrix products, arithmetic and copies ran while one was open for 0% of the time, Pallas kernels for 19%

profile of v1, /device:TPU:18, one launch (start us, length us, event | category | flops | bytes accessed | tf_op | source)
XLA Modules:
  0.0 151.4 jit_solution(8167614769373335546)
XLA Ops:
  0.0 2.7 %collective-permute-start.4 = (bf16[512,1536]{1,0:T(8,128)(2,1)}, bf16[512,1536]{1,0:T(8,128)(2,1)}, u32[]{:S(2)}, u32[]{:S(2)}) collective-permute-start(bf16[512,1536]{1,0:T(8,128)(2,1)} %bitcast.8), channel_id=1, source_target_pairs={{1,2},{3,4},{5,6},{7,8},{9,10},{11,12},{13,14},{2,1},{4,3},{6,5},{... | collective-permute-start | bytes 4718600 | tf_op jit(solution)/shard_map/ppermute | solution.py:29
  2.8 3.7 %collective-permute-start.5 = (bf16[512,1536]{1,0:T(8,128)(2,1)}, bf16[512,1536]{1,0:T(8,128)(2,1)}, u32[]{:S(2)}, u32[]{:S(2)}) collective-permute-start(bf16[512,1536]{1,0:T(8,128)(2,1)} %bitcast.12), channel_id=1, source_target_pairs={{1,2},{3,4},{5,6},{7,8},{9,10},{11,12},{13,14},{2,1},{4,3},{6,5},{... | collective-permute-start | bytes 4718600 | tf_op jit(solution)/shard_map/ppermute | solution.py:29
  6.5 0.1 collective-permute-start.7
  6.6 0.5 collective-permute-start.8
  7.0 16.0 %collective-permute-done.4.keys_ref.refs_0_ = bf16[512,1536]{1,0:T(8,128)(2,1)} collective-permute-done((bf16[512,1536]{1,0:T(8,128)(2,1)}, bf16[512,1536]{1,0:T(8,128)(2,1)}, u32[]{:S(2)}, u32[]{:S(2)}) %collective-permute-start.4) | collective-permute-done | bytes 1572896 | tf_op jit(solution)/shard_map/ppermute | solution.py:29
  23.0 16.9 %collective-permute-done.5.values_ref.refs_1_ = bf16[512,1536]{1,0:T(8,128)(2,1)} collective-permute-done((bf16[512,1536]{1,0:T(8,128)(2,1)}, bf16[512,1536]{1,0:T(8,128)(2,1)}, u32[]{:S(2)}, u32[]{:S(2)}) %collective-permute-start.5) | collective-permute-done | bytes 1572896 | tf_op jit(solution)/shard_map/ppermute | solution.py:29
  39.9 2.8 %shard_map.56 = bf16[128,3072]{1,0:T(8,128)(2,1)} custom-call(s32[6,16]{1,0:T(8,128)} %bitcast.16, bf16[512,1536]{1,0:T(8,128)(2,1)} %collective-permute-done.4.keys_ref.refs_0_, bf16[512,1536]{1,0:T(8,128)(2,1)} %collective-permute-done.5.values_ref.refs_1_), custom_call_target="tpu_custom_call" | custom-call | bytes 1572864 | tf_op jit(solution)/shard_map/pallas_call | solution.py:67
  42.7 32.7 %collective-permute-start.6 = (bf16[128,3072]{1,0:T(8,128)(2,1)}, bf16[128,3072]{1,0:T(8,128)(2,1)}, u32[]{:S(2)}, u32[]{:S(2)}) collective-permute-start(bf16[128,3072]{1,0:T(8,128)(2,1)} %shard_map.56), channel_id=1, source_target_pairs={{0,1},{2,3},{4,5},{6,7},{8,9},{10,11},{12,13},{14,15},{1,0},{3,2},... | collective-permute-start | bytes 2359304 | tf_op jit(solution)/shard_map/ppermute | solution.py:29
  75.4 4.3 %shard_map.55 = (bf16[128,3072]{1,0:T(8,128)(2,1)}, bf16[128,3072]{1,0:T(8,128)(2,1)}, bf16[128,3072]{1,0:T(8,128)(2,1)}, bf16[128,3072]{1,0:T(8,128)(2,1)}) custom-call(s32[6,16]{1,0:T(8,128)} %bitcast.17, bf16[512,1536]{1,0:T(8,128)(2,1)} %bitcast.10, bf16[512,1536]{1,0:T(8,128)(2,1)} %bitcast.14), custom_call_target="tpu_custom_call" | custom-call | bytes 6291456 | tf_op jit(solution)/shard_map/pallas_call | solution.py:67
  79.7 0.1 collective-permute-start
  79.7 3.8 %collective-permute-start.1 = (bf16[128,3072]{1,0:T(8,128)(2,1)}, bf16[128,3072]{1,0:T(8,128)(2,1)}, u32[]{:S(2)}, u32[]{:S(2)}) collective-permute-start(bf16[128,3072]{1,0:T(8,128)(2,1)} %get-tuple-element.14), channel_id=1, source_target_pairs={{0,4},{1,5},{2,6},{3,7},{4,8},{5,9},{6,10},{7,11},{8,12},{9,13},{1... | collective-permute-start | bytes 2359304 | tf_op jit(solution)/shard_map/ppermute | solution.py:29
  83.6 0.0 collective-permute-done.7.refs_2_
  83.6 3.2 %collective-permute-start.2 = (bf16[128,3072]{1,0:T(8,128)(2,1)}, bf16[128,3072]{1,0:T(8,128)(2,1)}, u32[]{:S(2)}, u32[]{:S(2)}) collective-permute-start(bf16[128,3072]{1,0:T(8,128)(2,1)} %get-tuple-element.15), channel_id=1, source_target_pairs={{4,0},{5,1},{6,2},{7,3},{8,4},{9,5},{10,6},{11,7},{12,8},{13,9},{1... | collective-permute-start | bytes 2359304 | tf_op jit(solution)/shard_map/ppermute | solution.py:29
  86.7 0.0 collective-permute-done.8.refs_3_
  86.8 2.7 %collective-permute-start.3 = (bf16[128,3072]{1,0:T(8,128)(2,1)}, bf16[128,3072]{1,0:T(8,128)(2,1)}, u32[]{:S(2)}, u32[]{:S(2)}) collective-permute-start(bf16[128,3072]{1,0:T(8,128)(2,1)} %get-tuple-element.16), channel_id=1, source_target_pairs={{0,2},{2,4},{4,6},{6,8},{8,10},{10,12},{12,14},{3,1},{5,3},{7,5},{... | collective-permute-start | bytes 2359304 | tf_op jit(solution)/shard_map/ppermute | solution.py:29
  90.1 12.1 %shard_map.57 = (f32[1536,512]{1,0:T(8,128)}, f32[96,512]{1,0:T(8,128)}) custom-call(s32[1]{0:T(128)S(6)} %copy.6.window_ref, bf16[512,1536]{1,0:T(8,128)(2,1)} %bitcast.5, bf16[512,1536]{1,0:T(8,128)(2,1)} %bitcast.11, bf16[512,1536]{1,0:T(8,128)(2,1)} %bitcast.15, bf16[512,1536]{1,0:T(8,128)(2,1)} %collective-permute-done.7.refs_2_, ...), custom_call_target="tpu_custom_call" | custom-call | flops 3221225472 | bytes 9437184 | tf_op jit(solution)/shard_map/pallas_call | solution.py:195
  102.3 0.0 collective-permute-done.6.refs_2_.refs_3_
  102.3 9.7 %shard_map.58 = (f32[1536,512]{1,0:T(8,128)}, f32[96,512]{1,0:T(8,128)}) custom-call(s32[1]{0:T(128)S(6)} %copy.6.window_ref, bf16[512,1536]{1,0:T(8,128)(2,1)} %bitcast.6, bf16[512,1536]{1,0:T(8,128)(2,1)} %collective-permute-done.4.keys_ref.refs_0_, bf16[512,1536]{1,0:T(8,128)(2,1)} %collective-permute-done.5.values_ref.refs_1_, ...), custom_call_target="tpu_custom_call" | custom-call | flops 2013265920 | bytes 10223616 | tf_op jit(solution)/shard_map/pallas_call | solution.py:195
  112.0 2.9 %collective-permute-done.refs_0_.refs_1_ = bf16[128,3072]{1,0:T(8,128)(2,1)} collective-permute-done((bf16[128,3072]{1,0:T(8,128)(2,1)}, bf16[128,3072]{1,0:T(8,128)(2,1)}, u32[]{:S(2)}, u32[]{:S(2)}) %collective-permute-start) | collective-permute-done | bytes 786464 | tf_op jit(solution)/shard_map/ppermute | solution.py:29
  114.9 19.4 %collective-permute-done.1.refs_2_.refs_3_ = bf16[128,3072]{1,0:T(8,128)(2,1)} collective-permute-done((bf16[128,3072]{1,0:T(8,128)(2,1)}, bf16[128,3072]{1,0:T(8,128)(2,1)}, u32[]{:S(2)}, u32[]{:S(2)}) %collective-permute-start.1) | collective-permute-done | bytes 786464 | tf_op jit(solution)/shard_map/ppermute | solution.py:29
  134.3 0.0 collective-permute-done.2.refs_4_.refs_5_
  134.3 8.2 %collective-permute-done.3.refs_6_.refs_7_ = bf16[128,3072]{1,0:T(8,128)(2,1)} collective-permute-done((bf16[128,3072]{1,0:T(8,128)(2,1)}, bf16[128,3072]{1,0:T(8,128)(2,1)}, u32[]{:S(2)}, u32[]{:S(2)}) %collective-permute-start.3) | collective-permute-done | bytes 786464 | tf_op jit(solution)/shard_map/ppermute | solution.py:29
  142.4 9.0 %shard_map.59 = bf16[512,1536]{1,0:T(8,128)(2,1)} custom-call(s32[1]{0:T(128)S(6)} %copy.6.window_ref, bf16[512,1536]{1,0:T(8,128)(2,1)} %bitcast.7, bf16[128,3072]{1,0:T(8,128)(2,1)} %collective-permute-done.refs_0_.refs_1_, bf16[128,3072]{1,0:T(8,128)(2,1)} %collective-permute-done.refs_0_.refs_1_, ...), custom_call_target="tpu_custom_call" | custom-call | flops 1610612736 | bytes 9437184 | tf_op jit(solution)/shard_map/pallas_call | solution.py:195
Async XLA Ops:
  0.0 23.0 %collective-permute-start.4 = (bf16[512,1536]{1,0:T(8,128)(2,1)}, bf16[512,1536]{1,0:T(8,128)(2,1)}, u32[]{:S(2)}, u32[]{:S(2)}) collective-permute-start(bf16[512,1536]{1,0:T(8,128)(2,1)} %bitcast.8), channel_id=1, source_target_pairs={{1,2},{3,4},{5,6},{7,8},{9,10},{11,12},{13,14},{2,1},{4,3},{6,5},{... | collective-permute-start | bytes 4718600 | tf_op jit(solution)/shard_map/ppermute | solution.py:29
  2.8 37.1 %collective-permute-start.5 = (bf16[512,1536]{1,0:T(8,128)(2,1)}, bf16[512,1536]{1,0:T(8,128)(2,1)}, u32[]{:S(2)}, u32[]{:S(2)}) collective-permute-start(bf16[512,1536]{1,0:T(8,128)(2,1)} %bitcast.12), channel_id=1, source_target_pairs={{1,2},{3,4},{5,6},{7,8},{9,10},{11,12},{13,14},{2,1},{4,3},{6,5},{... | collective-permute-start | bytes 4718600 | tf_op jit(solution)/shard_map/ppermute | solution.py:29
  6.5 77.1 %collective-permute-start.7 = (bf16[512,1536]{1,0:T(8,128)(2,1)}, bf16[512,1536]{1,0:T(8,128)(2,1)}, u32[]{:S(2)}, u32[]{:S(2)}) collective-permute-start(bf16[512,1536]{1,0:T(8,128)(2,1)} %bitcast.9), channel_id=1, source_target_pairs={{0,1},{2,3},{4,5},{6,7},{8,9},{10,11},{12,13},{14,15},{1,0},{3,2},... | collective-permute-start | bytes 4718600 | tf_op jit(solution)/shard_map/ppermute | solution.py:29
  6.6 80.2 %collective-permute-start.8 = (bf16[512,1536]{1,0:T(8,128)(2,1)}, bf16[512,1536]{1,0:T(8,128)(2,1)}, u32[]{:S(2)}, u32[]{:S(2)}) collective-permute-start(bf16[512,1536]{1,0:T(8,128)(2,1)} %bitcast.13), channel_id=1, source_target_pairs={{0,1},{2,3},{4,5},{6,7},{8,9},{10,11},{12,13},{14,15},{1,0},{3,2},... | collective-permute-start | bytes 4718600 | tf_op jit(solution)/shard_map/ppermute | solution.py:29
  42.7 59.6 %collective-permute-start.6 = (bf16[128,3072]{1,0:T(8,128)(2,1)}, bf16[128,3072]{1,0:T(8,128)(2,1)}, u32[]{:S(2)}, u32[]{:S(2)}) collective-permute-start(bf16[128,3072]{1,0:T(8,128)(2,1)} %shard_map.56), channel_id=1, source_target_pairs={{0,1},{2,3},{4,5},{6,7},{8,9},{10,11},{12,13},{14,15},{1,0},{3,2},... | collective-permute-start | bytes 2359304 | tf_op jit(solution)/shard_map/ppermute | solution.py:29
  79.7 35.2 %collective-permute-start = (bf16[128,3072]{1,0:T(8,128)(2,1)}, bf16[128,3072]{1,0:T(8,128)(2,1)}, u32[]{:S(2)}, u32[]{:S(2)}) collective-permute-start(bf16[128,3072]{1,0:T(8,128)(2,1)} %get-tuple-element.13), channel_id=1, source_target_pairs={{0,8},{1,9},{2,10},{3,11},{4,12},{5,13},{6,14},{7,15},{8,0},{9,1},... | collective-permute-start | bytes 2359304 | tf_op jit(solution)/shard_map/ppermute | solution.py:29
  79.7 54.5 %collective-permute-start.1 = (bf16[128,3072]{1,0:T(8,128)(2,1)}, bf16[128,3072]{1,0:T(8,128)(2,1)}, u32[]{:S(2)}, u32[]{:S(2)}) collective-permute-start(bf16[128,3072]{1,0:T(8,128)(2,1)} %get-tuple-element.14), channel_id=1, source_target_pairs={{0,4},{1,5},{2,6},{3,7},{4,8},{5,9},{6,10},{7,11},{8,12},{9,13},{1... | collective-permute-start | bytes 2359304 | tf_op jit(solution)/shard_map/ppermute | solution.py:29
  83.6 50.7 %collective-permute-start.2 = (bf16[128,3072]{1,0:T(8,128)(2,1)}, bf16[128,3072]{1,0:T(8,128)(2,1)}, u32[]{:S(2)}, u32[]{:S(2)}) collective-permute-start(bf16[128,3072]{1,0:T(8,128)(2,1)} %get-tuple-element.15), channel_id=1, source_target_pairs={{4,0},{5,1},{6,2},{7,3},{8,4},{9,5},{10,6},{11,7},{12,8},{13,9},{1... | collective-permute-start | bytes 2359304 | tf_op jit(solution)/shard_map/ppermute | solution.py:29
  86.8 55.7 %collective-permute-start.3 = (bf16[128,3072]{1,0:T(8,128)(2,1)}, bf16[128,3072]{1,0:T(8,128)(2,1)}, u32[]{:S(2)}, u32[]{:S(2)}) collective-permute-start(bf16[128,3072]{1,0:T(8,128)(2,1)} %get-tuple-element.16), channel_id=1, source_target_pairs={{0,2},{2,4},{4,6},{6,8},{8,10},{10,12},{12,14},{3,1},{5,3},{7,5},{... | collective-permute-start | bytes 2359304 | tf_op jit(solution)/shard_map/ppermute | solution.py:29

commit v2 on v1

--- a/solution.py
+++ b/solution.py
@@ -81,13 +81,15 @@
     )(picks.T, keys, values)
 
 
-def attend_kernel(kinds, together, first, last, window_ref, q_ref, *refs):
+def attend_kernel(kinds, together, first, last, onto, window_ref, q_ref, *refs):
     count = len(kinds)
     sources = [(refs[2 * i], refs[2 * i + 1]) for i in range(count)]
     refs = refs[2 * count :]
     if not first:
         acc_in, stat_in = refs[:2]
         refs = refs[2:]
+    if onto:
+        refs = refs[1:]
     if last:
         out_ref, bias_ref, class_ref, turned_ref = refs
     else:
@@ -159,41 +161,50 @@
             stat_out[8 * head + 1 : 8 * head + 2, :] = norm
 
 
-def attend(window, query, sources, state, last):
+def attend(window, query, sources, part, state, last, target=None):
     tokens, width = query.shape
-    heads = width // HD
-    together = next(n for n in (3, 2, 1) if heads % n == 0)
+    first_head, heads = part
+    together = next(n for n in (3, 2, 1) if heads % n == 0 and first_head % n == 0)
     kinds = tuple(source[4:] for source in sources)
 
     def columns(rows, base):
         return pl.BlockSpec((rows, HD * together), lambda h, window: (0, base // together + h))
 
-    specs, operands = [columns(tokens, 0)], [query]
+    def state_specs(base):
+        return [
+            pl.BlockSpec((HD * together, tokens), lambda h, window: (base // together + h, 0)),
+            pl.BlockSpec((8 * together, tokens), lambda h, window: (base // together + h, 0)),
+        ]
+
+    specs, operands = [columns(tokens, first_head)], [query]
     keys_count = 0
     for key, key_base, value, value_base, _, _ in sources:
         specs += [columns(key.shape[0], key_base), columns(key.shape[0], value_base)]
         operands += [key, value]
         keys_count += key.shape[0]
-    state_specs = [
-        pl.BlockSpec((HD * together, tokens), lambda h, window: (h, 0)),
-        pl.BlockSpec((8 * together, tokens), lambda h, window: (h, 0)),
-    ]
-    moved_bytes = 2 * (tokens + 2 * keys_count) * width
+    moved_bytes = 2 * (tokens + 2 * keys_count) * heads * HD
     if state is not None:
-        specs += state_specs
-        operands += list(state)
-        moved_bytes += 4 * tokens * width
+        specs += state_specs(state[2])
+        operands += state[:2]
+        moved_bytes += 4 * tokens * heads * HD
+    aliases = {}
     if last:
         out_shape = jax.ShapeDtypeStruct((tokens, width), jnp.bfloat16)
-        out_specs = columns(tokens, 0)
+        out_specs = columns(tokens, first_head)
+        if target is not None:
+            aliases = {1 + len(operands): 0}
+            specs.append(pl.BlockSpec(memory_space=pl.ANY))
+            operands.append(target)
     else:
         out_shape = [
-            jax.ShapeDtypeStruct((width, tokens), jnp.float32),
+            jax.ShapeDtypeStruct((HD * heads, tokens), jnp.float32),
             jax.ShapeDtypeStruct((8 * heads, tokens), jnp.float32),
         ]
-        out_specs = state_specs
+        out_specs = state_specs(0)
     return pl.pallas_call(
-        functools.partial(attend_kernel, kinds, together, state is None, last),
+        functools.partial(
+            attend_kernel, kinds, together, state is None, last, target is not None
+        ),
         out_shape=out_shape,
         grid_spec=pltpu.PrefetchScalarGridSpec(
             num_scalar_prefetch=1,
@@ -206,10 +217,11 @@
                 pltpu.VMEM((together, HD + ONES, keys_count), jnp.bfloat16),
             ],
         ),
+        input_output_aliases=aliases,
         compiler_params=pltpu.CompilerParams(vmem_limit_bytes=67_043_328),
         cost_estimate=pl.CostEstimate(
-            flops=4 * tokens * keys_count * width,
-            bytes_accessed=moved_bytes + 2 * tokens * width,
+            flops=4 * tokens * keys_count * heads * HD,
+            bytes_accessed=moved_bytes + 2 * tokens * heads * HD,
             transcendentals=tokens * keys_count * heads,
         ),
     )(window, *operands)
@@ -230,9 +242,14 @@
 
     outward = [(1, is_odd), (-1, is_even)]
     inward = [(1, is_even), (-1, is_odd)]
-    beyond_keys = moved(keys, outward)
-    beyond_values = moved(values, outward)
-    beyond = [beyond_keys, beyond_values]
+    half_heads = heads // 2
+    halves = [(0, half_heads), (half_heads, heads - half_heads)]
+    beyond = []
+    for half, (start, count) in enumerate(halves):
+        part = slice(start * HD, (start + count) * HD)
+        beyond_keys = moved(keys[:, part], outward)
+        beyond_values = moved(values[:, part], outward)
+        beyond.append((beyond_keys, beyond_values))
 
     far = []
     for column in sorted(range(len(offsets)), key=lambda c: -abs(offsets[c])):
@@ -287,20 +304,33 @@
     def near_there(position):
         return there(beyond_of(position))
 
+    def ahead_there(position):
+        return there(position + 2 - 4 * (position % 2))
+
     own = [(keys, 0, values, 0, True, always), (mate_keys, 0, mate_values, 0, True, always)]
-    state = attend(win_rows, query, own, None, False)
-    nearby = [(beyond[0], 0, beyond[1], 0, True, near_there)]
-    if shared:
-        (handed,) = gather(far_picks, *beyond, [partner], frames)
-        handed = moved(handed, inward)
-        nearby.append(
-            (handed, 0, handed, heads, False, lambda p: there(p + 2 - 4 * (p % 2)))
-        )
-    state = attend(win_rows, query, nearby, state, False)
-    distant = [
-        (block, 0, block, heads, False, there) for block, (_, _, there) in zip(arrived, far)
-    ]
-    return attend(win_rows, query, distant, state, True)[None]
+    state = attend(win_rows, query, own, (0, heads), None, False)
+
+    def nearby(half, state, last, target):
+        keys, values = beyond[half]
+        sources = [(keys, 0, values, 0, True, near_there)]
+        if shared:
+            (block,) = gather(far_picks, keys, values, [partner], frames)
+            block = moved(block, inward)
+            sources.append((block, 0, block, halves[half][1], False, ahead_there))
+        return attend(win_rows, query, sources, halves[half], state, last, target)
+
+    def distant(half, state, last):
+        start = halves[half][0]
+        sources = [
+            (block, start, block, heads + start, False, there)
+            for block, (_, _, there) in zip(arrived, far)
+        ]
+        return attend(win_rows, query, sources, halves[half], state, last)
+
+    low = nearby(0, (*state, 0), False, None)
+    high = distant(1, (*state, half_heads), False)
+    out = distant(0, (*low, 0), True)
+    return nearby(1, (*high, 0), True, out)[None]
 
 
 def solution(mesh):

time: 152 us -> 131 us (0.86)
  the two profiles are of different devices: /device:TPU:18 before, /device:TPU:15 now
where the time goes in v2:
time: 131 us
  waiting for transfers between devices  56.4 us (43%)
  Pallas kernels  45.2 us (35%)
  starting transfers between devices  22.9 us (17%)
  local copies, waits for them, and re-layouts  5.2 us (4%)
    ppermute x12, waiting for transfers between devices, moved(): return lax.ppermute(value, 'frame', pairs)  56.4 us
    pallas_call x5, Pallas kernels, attend(): pl.pallas_call(functools.partial(attend_kernel, kinds, together, state is...  35.7 us
    ppermute x12, starting transfers between devices, moved(): return lax.ppermute(value, 'frame', pairs)  22.9 us
    pallas_call x3, Pallas kernels, gather(): pl.pallas_call(functools.partial(gather_kernel, readers, frames), out_sha...  9.47 us
  transfers between devices with their start and end apart: 12, of which 4 were waited for; matrix products, arithmetic and copies ran while one was open for 2% of the time, Pallas kernels for 30%

profile of v2, /device:TPU:15, one launch (start us, length us, event | category | flops | bytes accessed | tf_op | source)
XLA Modules:
  0.0 130.5 jit_solution(2638284107828653686)
XLA Ops:
  0.0 2.6 %fusion = (bf16[512,768]{1,0:T(8,128)(2,1)}, bf16[512,768]{1,0:T(8,128)(2,1)}) fusion(bf16[512,1536]{1,0:T(8,128)(2,1)} %bitcast.2.values_ref.refs_1_), kind=kLoop, calls=%fused_computation | loop fusion | bytes 3145728 | tf_op jit(solution)/shard_map/slice | solution.py:251
  2.6 3.7 %collective-permute-start.10 = (bf16[512,768]{1,0:T(8,128)(2,1)}, bf16[512,768]{1,0:T(8,128)(2,1)}, u32[]{:S(2)}, u32[]{:S(2)}) collective-permute-start(bf16[512,768]{1,0:T(8,128)(2,1)} %get-tuple-element.25), channel_id=1, source_target_pairs={{1,2},{3,4},{5,6},{7,8},{9,10},{11,12},{13,14},{2,1},{4,3},{6,5},{... | collective-permute-start | bytes 2359304 | tf_op jit(solution)/shard_map/ppermute | solution.py:29
  6.3 2.6 %fusion.1 = (bf16[512,768]{1,0:T(8,128)(2,1)}, bf16[512,768]{1,0:T(8,128)(2,1)}) fusion(bf16[512,1536]{1,0:T(8,128)(2,1)} %bitcast.1.keys_ref.refs_0_), kind=kLoop, calls=%fused_computation.1 | loop fusion | bytes 3145728 | tf_op jit(solution)/shard_map/slice | solution.py:250
  8.9 2.7 %collective-permute-start.9 = (bf16[512,768]{1,0:T(8,128)(2,1)}, bf16[512,768]{1,0:T(8,128)(2,1)}, u32[]{:S(2)}, u32[]{:S(2)}) collective-permute-start(bf16[512,768]{1,0:T(8,128)(2,1)} %get-tuple-element.27), channel_id=1, source_target_pairs={{1,2},{3,4},{5,6},{7,8},{9,10},{11,12},{13,14},{2,1},{4,3},{6,5},{... | collective-permute-start | bytes 2359304 | tf_op jit(solution)/shard_map/ppermute | solution.py:29
  11.7 0.1 collective-permute-start.7
  11.7 0.5 collective-permute-start.8
  12.2 4.4 %shard_map.56 = (bf16[128,3072]{1,0:T(8,128)(2,1)}, bf16[128,3072]{1,0:T(8,128)(2,1)}, bf16[128,3072]{1,0:T(8,128)(2,1)}, bf16[128,3072]{1,0:T(8,128)(2,1)}) custom-call(s32[6,16]{1,0:T(8,128)} %bitcast.10, bf16[512,1536]{1,0:T(8,128)(2,1)} %bitcast.1.keys_ref.refs_0_, bf16[512,1536]{1,0:T(8,128)(2,1)} %bitcast.2.values_ref.refs_1_), custom_call_target="tpu_custom_call" | custom-call | bytes 6291456 | tf_op jit(solution)/shard_map/pallas_call | solution.py:67
  16.6 1.7 %collective-permute-start.3 = (bf16[128,3072]{1,0:T(8,128)(2,1)}, bf16[128,3072]{1,0:T(8,128)(2,1)}, u32[]{:S(2)}, u32[]{:S(2)}) collective-permute-start(bf16[128,3072]{1,0:T(8,128)(2,1)} %get-tuple-element.15), channel_id=1, source_target_pairs={{0,8},{1,9},{2,10},{3,11},{4,12},{5,13},{6,14},{7,15},{8,0},{9,1},... | collective-permute-start | bytes 2359304 | tf_op jit(solution)/shard_map/ppermute | solution.py:29
  18.3 0.0 collective-permute-done.10.values_ref.refs_1_
  18.3 2.6 %collective-permute-start = (bf16[512,768]{1,0:T(8,128)(2,1)}, bf16[512,768]{1,0:T(8,128)(2,1)}, u32[]{:S(2)}, u32[]{:S(2)}) collective-permute-start(bf16[512,768]{1,0:T(8,128)(2,1)} %get-tuple-element.28), channel_id=1, source_target_pairs={{1,2},{3,4},{5,6},{7,8},{9,10},{11,12},{13,14},{2,1},{4,3},{6,5},{... | collective-permute-start | bytes 2359304 | tf_op jit(solution)/shard_map/ppermute | solution.py:29
  20.9 27.7 %collective-permute-done.9.keys_ref.refs_0_ = bf16[512,768]{1,0:T(8,128)(2,1)} collective-permute-done((bf16[512,768]{1,0:T(8,128)(2,1)}, bf16[512,768]{1,0:T(8,128)(2,1)}, u32[]{:S(2)}, u32[]{:S(2)}) %collective-permute-start.9) | collective-permute-done | bytes 786464 | tf_op jit(solution)/shard_map/ppermute | solution.py:29
  48.6 1.9 %collective-permute-start.1 = (bf16[512,768]{1,0:T(8,128)(2,1)}, bf16[512,768]{1,0:T(8,128)(2,1)}, u32[]{:S(2)}, u32[]{:S(2)}) collective-permute-start(bf16[512,768]{1,0:T(8,128)(2,1)} %get-tuple-element.26), channel_id=1, source_target_pairs={{1,2},{3,4},{5,6},{7,8},{9,10},{11,12},{13,14},{2,1},{4,3},{6,5},{... | collective-permute-start | bytes 2359304 | tf_op jit(solution)/shard_map/ppermute | solution.py:29
  50.5 7.9 %collective-permute-done.3.refs_0_.refs_1_ = bf16[128,3072]{1,0:T(8,128)(2,1)} collective-permute-done((bf16[128,3072]{1,0:T(8,128)(2,1)}, bf16[128,3072]{1,0:T(8,128)(2,1)}, u32[]{:S(2)}, u32[]{:S(2)}) %collective-permute-start.3) | collective-permute-done | bytes 786464 | tf_op jit(solution)/shard_map/ppermute | solution.py:29
  58.4 1.9 %collective-permute-start.4 = (bf16[128,3072]{1,0:T(8,128)(2,1)}, bf16[128,3072]{1,0:T(8,128)(2,1)}, u32[]{:S(2)}, u32[]{:S(2)}) collective-permute-start(bf16[128,3072]{1,0:T(8,128)(2,1)} %get-tuple-element.16), channel_id=1, source_target_pairs={{0,4},{1,5},{2,6},{3,7},{4,8},{5,9},{6,10},{7,11},{8,12},{9,13},{1... | collective-permute-start | bytes 2359304 | tf_op jit(solution)/shard_map/ppermute | solution.py:29
  60.3 14.3 %collective-permute-done.keys_ref.refs_0_ = bf16[512,768]{1,0:T(8,128)(2,1)} collective-permute-done((bf16[512,768]{1,0:T(8,128)(2,1)}, bf16[512,768]{1,0:T(8,128)(2,1)}, u32[]{:S(2)}, u32[]{:S(2)}) %collective-permute-start) | collective-permute-done | bytes 786464 | tf_op jit(solution)/shard_map/ppermute | solution.py:29
  74.6 1.9 %collective-permute-start.5 = (bf16[128,3072]{1,0:T(8,128)(2,1)}, bf16[128,3072]{1,0:T(8,128)(2,1)}, u32[]{:S(2)}, u32[]{:S(2)}) collective-permute-start(bf16[128,3072]{1,0:T(8,128)(2,1)} %get-tuple-element.17), channel_id=1, source_target_pairs={{4,0},{5,1},{6,2},{7,3},{8,4},{9,5},{10,6},{11,7},{12,8},{13,9},{1... | collective-permute-start | bytes 2359304 | tf_op jit(solution)/shard_map/ppermute | solution.py:29
  76.5 6.6 %collective-permute-done.1.values_ref.refs_1_ = bf16[512,768]{1,0:T(8,128)(2,1)} collective-permute-done((bf16[512,768]{1,0:T(8,128)(2,1)}, bf16[512,768]{1,0:T(8,128)(2,1)}, u32[]{:S(2)}, u32[]{:S(2)}) %collective-permute-start.1) | collective-permute-done | bytes 786464 | tf_op jit(solution)/shard_map/ppermute | solution.py:29
  83.1 1.9 %collective-permute-start.6 = (bf16[128,3072]{1,0:T(8,128)(2,1)}, bf16[128,3072]{1,0:T(8,128)(2,1)}, u32[]{:S(2)}, u32[]{:S(2)}) collective-permute-start(bf16[128,3072]{1,0:T(8,128)(2,1)} %get-tuple-element.18), channel_id=1, source_target_pairs={{0,2},{2,4},{4,6},{6,8},{8,10},{10,12},{12,14},{3,1},{5,3},{7,5},{... | collective-permute-start | bytes 2359304 | tf_op jit(solution)/shard_map/ppermute | solution.py:29
  85.0 2.5 %shard_map.59 = bf16[128,1536]{1,0:T(8,128)(2,1)} custom-call(s32[6,16]{1,0:T(8,128)} %bitcast.11, bf16[512,768]{1,0:T(8,128)(2,1)} %collective-permute-done.9.keys_ref.refs_0_, bf16[512,768]{1,0:T(8,128)(2,1)} %collective-permute-done.10.values_ref.refs_1_), custom_call_target="tpu_custom_call" | custom-call | bytes 786432 | tf_op jit(solution)/shard_map/pallas_call | solution.py:67
  87.5 0.0 collective-permute-done.7.refs_2_
  87.5 3.9 %collective-permute-start.11 = (bf16[128,1536]{1,0:T(8,128)(2,1)}, bf16[128,1536]{1,0:T(8,128)(2,1)}, u32[]{:S(2)}, u32[]{:S(2)}) collective-permute-start(bf16[128,1536]{1,0:T(8,128)(2,1)} %shard_map.59), channel_id=1, source_target_pairs={{0,1},{2,3},{4,5},{6,7},{8,9},{10,11},{12,13},{14,15},{1,0},{3,2},... | collective-permute-start | bytes 1179656 | tf_op jit(solution)/shard_map/ppermute | solution.py:29
  92.1 2.6 %shard_map.55 = bf16[128,1536]{1,0:T(8,128)(2,1)} custom-call(s32[6,16]{1,0:T(8,128)} %bitcast.12, bf16[512,768]{1,0:T(8,128)(2,1)} %collective-permute-done.keys_ref.refs_0_, bf16[512,768]{1,0:T(8,128)(2,1)} %collective-permute-done.1.values_ref.refs_1_), custom_call_target="tpu_custom_call" | custom-call | bytes 786432 | tf_op jit(solution)/shard_map/pallas_call | solution.py:67
  94.6 0.0 collective-permute-done.8.refs_3_
  94.7 0.1 collective-permute-start.2
  94.7 12.2 %shard_map.57 = (f32[1536,512]{1,0:T(8,128)}, f32[96,512]{1,0:T(8,128)}) custom-call(s32[1]{0:T(128)S(6)} %copy.8.window_ref, bf16[512,1536]{1,0:T(8,128)(2,1)} %bitcast.5, bf16[512,1536]{1,0:T(8,128)(2,1)} %bitcast.1.keys_ref.refs_0_, bf16[512,1536]{1,0:T(8,128)(2,1)} %bitcast.2.values_ref.refs_1_, bf16[512,1536]{1,0:T(8,128)(2,1)} %collective-permute-done.7.refs_2_, ...), custom_call_target="tpu_custom_call" | custom-call | flops 3221225472 | bytes 9437184 | tf_op jit(solution)/shard_map/pallas_call | solution.py:204
  106.9 0.0 collective-permute-done.4.refs_2_.refs_3_
  106.9 0.0 collective-permute-done.5.refs_4_.refs_5_
  106.9 0.0 collective-permute-done.6.refs_6_.refs_7_
  106.9 5.6 %shard_map.58 = (f32[768,512]{1,0:T(8,128)}, f32[48,512]{1,0:T(8,128)}) custom-call(s32[1]{0:T(128)S(6)} %copy.8.window_ref, bf16[512,1536]{1,0:T(8,128)(2,1)} %bitcast.6, bf16[128,3072]{1,0:T(8,128)(2,1)} %collective-permute-done.3.refs_0_.refs_1_, bf16[128,3072]{1,0:T(8,128)(2,1)} %collective-permute-done.3.refs_0_.refs_1_, ...), custom_call_target="tpu_custom_call" | custom-call | flops 805306368 | bytes 4718592 | tf_op jit(solution)/shard_map/pallas_call | solution.py:204
  112.5 0.0 collective-permute-done.11.refs_2_.refs_3_
  112.6 6.1 %shard_map.60 = (f32[768,512]{1,0:T(8,128)}, f32[48,512]{1,0:T(8,128)}) custom-call(s32[1]{0:T(128)S(6)} %copy.8.window_ref, bf16[512,1536]{1,0:T(8,128)(2,1)} %bitcast.7, bf16[512,768]{1,0:T(8,128)(2,1)} %collective-permute-done.9.keys_ref.refs_0_, bf16[512,768]{1,0:T(8,128)(2,1)} %collective-permute-done.10.values_ref.refs_1_, ...), custom_call_target="tpu_custom_call" | custom-call | flops 1006632960 | bytes 5111808 | tf_op jit(solution)/shard_map/pallas_call | solution.py:204
  118.7 5.6 %shard_map.61.refs_6_ = bf16[512,1536]{1,0:T(8,128)(2,1)} custom-call(s32[1]{0:T(128)S(6)} %copy.8.window_ref, bf16[512,1536]{1,0:T(8,128)(2,1)} %bitcast.8, bf16[128,3072]{1,0:T(8,128)(2,1)} %collective-permute-done.3.refs_0_.refs_1_, bf16[128,3072]{1,0:T(8,128)(2,1)} %collective-permute-done.3.refs_0_.refs_1_, ...), custom_call_target="tpu_custom_call" | custom-call | flops 805306368 | bytes 4718592 | tf_op jit(solution)/shard_map/pallas_call | solution.py:204
  124.3 0.0 collective-permute-done.2.refs_2_.refs_3_
  124.3 6.2 %shard_map.62 = bf16[512,1536]{1,0:T(8,128)(2,1)} custom-call(s32[1]{0:T(128)S(6)} %copy.8.window_ref, bf16[512,1536]{1,0:T(8,128)(2,1)} %bitcast.9, bf16[512,768]{1,0:T(8,128)(2,1)} %collective-permute-done.keys_ref.refs_0_, bf16[512,768]{1,0:T(8,128)(2,1)} %collective-permute-done.1.values_ref.refs_1_, ...), custom_call_target="tpu_custom_call", output_to_operand_aliasing={{}: (8, {})} | custom-call | flops 1006632960 | bytes 5111808 | tf_op jit(solution)/shard_map/pallas_call | solution.py:204
Async XLA Ops:
  2.6 15.7 %collective-permute-start.10 = (bf16[512,768]{1,0:T(8,128)(2,1)}, bf16[512,768]{1,0:T(8,128)(2,1)}, u32[]{:S(2)}, u32[]{:S(2)}) collective-permute-start(bf16[512,768]{1,0:T(8,128)(2,1)} %get-tuple-element.25), channel_id=1, source_target_pairs={{1,2},{3,4},{5,6},{7,8},{9,10},{11,12},{13,14},{2,1},{4,3},{6,5},{... | collective-permute-start | bytes 2359304 | tf_op jit(solution)/shard_map/ppermute | solution.py:29
  8.9 39.7 %collective-permute-start.9 = (bf16[512,768]{1,0:T(8,128)(2,1)}, bf16[512,768]{1,0:T(8,128)(2,1)}, u32[]{:S(2)}, u32[]{:S(2)}) collective-permute-start(bf16[512,768]{1,0:T(8,128)(2,1)} %get-tuple-element.27), channel_id=1, source_target_pairs={{1,2},{3,4},{5,6},{7,8},{9,10},{11,12},{13,14},{2,1},{4,3},{6,5},{... | collective-permute-start | bytes 2359304 | tf_op jit(solution)/shard_map/ppermute | solution.py:29
  11.7 75.9 %collective-permute-start.7 = (bf16[512,1536]{1,0:T(8,128)(2,1)}, bf16[512,1536]{1,0:T(8,128)(2,1)}, u32[]{:S(2)}, u32[]{:S(2)}) collective-permute-start(bf16[512,1536]{1,0:T(8,128)(2,1)} %bitcast.1.keys_ref.refs_0_), channel_id=1, source_target_pairs={{0,1},{2,3},{4,5},{6,7},{8,9},{10,11},{12,13},{14,15},{1,0},{3,2},... | collective-permute-start | bytes 4718600 | tf_op jit(solution)/shard_map/ppermute | solution.py:29
  11.7 82.9 %collective-permute-start.8 = (bf16[512,1536]{1,0:T(8,128)(2,1)}, bf16[512,1536]{1,0:T(8,128)(2,1)}, u32[]{:S(2)}, u32[]{:S(2)}) collective-permute-start(bf16[512,1536]{1,0:T(8,128)(2,1)} %bitcast.2.values_ref.refs_1_), channel_id=1, source_target_pairs={{0,1},{2,3},{4,5},{6,7},{8,9},{10,11},{12,13},{14,15},{1,0},{3,2},... | collective-permute-start | bytes 4718600 | tf_op jit(solution)/shard_map/ppermute | solution.py:29
  16.6 41.8 %collective-permute-start.3 = (bf16[128,3072]{1,0:T(8,128)(2,1)}, bf16[128,3072]{1,0:T(8,128)(2,1)}, u32[]{:S(2)}, u32[]{:S(2)}) collective-permute-start(bf16[128,3072]{1,0:T(8,128)(2,1)} %get-tuple-element.15), channel_id=1, source_target_pairs={{0,8},{1,9},{2,10},{3,11},{4,12},{5,13},{6,14},{7,15},{8,0},{9,1},... | collective-permute-start | bytes 2359304 | tf_op jit(solution)/shard_map/ppermute | solution.py:29
  18.3 56.3 %collective-permute-start = (bf16[512,768]{1,0:T(8,128)(2,1)}, bf16[512,768]{1,0:T(8,128)(2,1)}, u32[]{:S(2)}, u32[]{:S(2)}) collective-permute-start(bf16[512,768]{1,0:T(8,128)(2,1)} %get-tuple-element.28), channel_id=1, source_target_pairs={{1,2},{3,4},{5,6},{7,8},{9,10},{11,12},{13,14},{2,1},{4,3},{6,5},{... | collective-permute-start | bytes 2359304 | tf_op jit(solution)/shard_map/ppermute | solution.py:29
  48.6 34.5 %collective-permute-start.1 = (bf16[512,768]{1,0:T(8,128)(2,1)}, bf16[512,768]{1,0:T(8,128)(2,1)}, u32[]{:S(2)}, u32[]{:S(2)}) collective-permute-start(bf16[512,768]{1,0:T(8,128)(2,1)} %get-tuple-element.26), channel_id=1, source_target_pairs={{1,2},{3,4},{5,6},{7,8},{9,10},{11,12},{13,14},{2,1},{4,3},{6,5},{... | collective-permute-start | bytes 2359304 | tf_op jit(solution)/shard_map/ppermute | solution.py:29
  58.4 48.5 %collective-permute-start.4 = (bf16[128,3072]{1,0:T(8,128)(2,1)}, bf16[128,3072]{1,0:T(8,128)(2,1)}, u32[]{:S(2)}, u32[]{:S(2)}) collective-permute-start(bf16[128,3072]{1,0:T(8,128)(2,1)} %get-tuple-element.16), channel_id=1, source_target_pairs={{0,4},{1,5},{2,6},{3,7},{4,8},{5,9},{6,10},{7,11},{8,12},{9,13},{1... | collective-permute-start | bytes 2359304 | tf_op jit(solution)/shard_map/ppermute | solution.py:29
  74.6 32.3 %collective-permute-start.5 = (bf16[128,3072]{1,0:T(8,128)(2,1)}, bf16[128,3072]{1,0:T(8,128)(2,1)}, u32[]{:S(2)}, u32[]{:S(2)}) collective-permute-start(bf16[128,3072]{1,0:T(8,128)(2,1)} %get-tuple-element.17), channel_id=1, source_target_pairs={{4,0},{5,1},{6,2},{7,3},{8,4},{9,5},{10,6},{11,7},{12,8},{13,9},{1... | collective-permute-start | bytes 2359304 | tf_op jit(solution)/shard_map/ppermute | solution.py:29
  83.1 23.8 %collective-permute-start.6 = (bf16[128,3072]{1,0:T(8,128)(2,1)}, bf16[128,3072]{1,0:T(8,128)(2,1)}, u32[]{:S(2)}, u32[]{:S(2)}) collective-permute-start(bf16[128,3072]{1,0:T(8,128)(2,1)} %get-tuple-element.18), channel_id=1, source_target_pairs={{0,2},{2,4},{4,6},{6,8},{8,10},{10,12},{12,14},{3,1},{5,3},{7,5},{... | collective-permute-start | bytes 2359304 | tf_op jit(solution)/shard_map/ppermute | solution.py:29
  87.5 25.0 %collective-permute-start.11 = (bf16[128,1536]{1,0:T(8,128)(2,1)}, bf16[128,1536]{1,0:T(8,128)(2,1)}, u32[]{:S(2)}, u32[]{:S(2)}) collective-permute-start(bf16[128,1536]{1,0:T(8,128)(2,1)} %shard_map.59), channel_id=1, source_target_pairs={{0,1},{2,3},{4,5},{6,7},{8,9},{10,11},{12,13},{14,15},{1,0},{3,2},... | collective-permute-start | bytes 1179656 | tf_op jit(solution)/shard_map/ppermute | solution.py:29
  94.7 29.7 %collective-permute-start.2 = (bf16[128,1536]{1,0:T(8,128)(2,1)}, bf16[128,1536]{1,0:T(8,128)(2,1)}, u32[]{:S(2)}, u32[]{:S(2)}) collective-permute-start(bf16[128,1536]{1,0:T(8,128)(2,1)} %shard_map.55), channel_id=1, source_target_pairs={{0,1},{2,3},{4,5},{6,7},{8,9},{10,11},{12,13},{14,15},{1,0},{3,2},... | collective-permute-start | bytes 1179656 | tf_op jit(solution)/shard_map/ppermute | solution.py:29

commit v3 on v1

--- a/solution.py
+++ b/solution.py
@@ -41,50 +41,59 @@
     return frame % 2 == 1
 
 
-def gather_kernel(readers, frames, picks_ref, keys_ref, values_ref, *refs):
-    outs, sems = refs[: len(readers)], refs[len(readers)]
-    width = keys_ref.shape[1]
+def gather_kernel(readers, frames, count, instead, picks_ref, *refs):
+    arrays, outs = refs[:count], refs[count : count + len(readers)]
+    sems = refs[count + len(readers)]
     position = lax.axis_index("frame")
-    copies = []
-    for slot, (reader_of, out) in enumerate(zip(readers, outs)):
-        reader, column = reader_of(position)
-        pick = picks_ref[column, jnp.clip(reader, 0, frames - 1)]
-        rows = pl.ds(pl.multiple_of(pick * SUB, SUB), SUB)
-        for half, source in enumerate((keys_ref, values_ref)):
-            target = out.at[:, pl.ds(half * width, width)]
-            copies.append(
-                pltpu.make_async_copy(source.at[rows, :], target, sems.at[2 * slot + half])
-            )
-    for copy in copies:
-        copy.start()
-    for copy in copies:
-        copy.wait()
-
-
-def gather(picks, keys, values, readers, frames):
-    width = keys.shape[1]
-    shape = (SUB, 2 * width)
+
+    def copy_all(arrays):
+        copies = []
+        for slot, (reader_of, out) in enumerate(zip(readers, outs)):
+            reader, column = reader_of(position)
+            pick = picks_ref[column, jnp.clip(reader, 0, frames - 1)]
+            rows = pl.ds(pl.multiple_of(pick * SUB, SUB), SUB)
+            start = 0
+            for which, source in enumerate(arrays):
+                target = out.at[:, pl.ds(start, source.shape[1])]
+                sem = sems.at[count * slot + which]
+                copies.append(pltpu.make_async_copy(source.at[rows, :], target, sem))
+                start += source.shape[1]
+        for copy in copies:
+            copy.start()
+        for copy in copies:
+            copy.wait()
+
+    if instead is None:
+        copy_all(arrays)
+    else:
+        pl.when(instead(position))(lambda: copy_all([*arrays[:-2], arrays[-1]]))
+        pl.when(jnp.logical_not(instead(position)))(lambda: copy_all(arrays[:-1]))
+
+
+def gather(picks, arrays, readers, frames, instead=None):
+    width = sum(array.shape[1] for array in (arrays if instead is None else arrays[:-1]))
     return pl.pallas_call(
-        functools.partial(gather_kernel, readers, frames),
-        out_shape=[jax.ShapeDtypeStruct(shape, keys.dtype) for _ in readers],
+        functools.partial(gather_kernel, readers, frames, len(arrays), instead),
+        out_shape=[jax.ShapeDtypeStruct((SUB, width), arrays[0].dtype) for _ in readers],
         in_specs=[
             pl.BlockSpec(memory_space=pltpu.SMEM),
-            pl.BlockSpec(memory_space=pltpu.HBM),
-            pl.BlockSpec(memory_space=pltpu.HBM),
+            *[pl.BlockSpec(memory_space=pltpu.HBM)] * len(arrays),
         ],
         out_specs=[pl.BlockSpec(memory_space=pltpu.VMEM) for _ in readers],
-        scratch_shapes=[pltpu.SemaphoreType.DMA((2 * len(readers),))],
+        scratch_shapes=[pltpu.SemaphoreType.DMA((len(arrays) * len(readers),))],
         compiler_params=pltpu.CompilerParams(vmem_limit_bytes=67_043_328),
         cost_estimate=pl.CostEstimate(
-            flops=0, bytes_accessed=8 * SUB * width * len(readers), transcendentals=0
+            flops=0, bytes_accessed=4 * SUB * width * len(readers), transcendentals=0
         ),
-    )(picks.T, keys, values)
+    )(picks.T, *arrays)
 
 
 def attend_kernel(kinds, together, first, last, window_ref, q_ref, *refs):
-    count = len(kinds)
-    sources = [(refs[2 * i], refs[2 * i + 1]) for i in range(count)]
-    refs = refs[2 * count :]
+    sources = []
+    for _, _, instead in kinds:
+        count = 2 if instead is None else 3
+        sources.append(refs[:count])
+        refs = refs[count:]
     if not first:
         acc_in, stat_in = refs[:2]
         refs = refs[2:]
@@ -93,16 +102,16 @@
     else:
         acc_out, stat_out, bias_ref, class_ref, turned_ref = refs
     tokens = q_ref.shape[0]
-    sizes = [key_ref.shape[0] for key_ref, _ in sources]
+    sizes = [source[0].shape[0] for source in sources]
+    position = lax.axis_index("frame")
 
     @pl.when(pl.program_id(0) == 0)
     def _():
-        position = lax.axis_index("frame")
         row = lax.broadcasted_iota(jnp.int32, (tokens, HD), 0) // COLS
         lane = lax.broadcasted_iota(jnp.int32, (tokens, HD), 1)
         bias = jnp.zeros((tokens, HD), jnp.float32)
         base, start = 0, 0
-        for (windowed, there), size in zip(kinds, sizes):
+        for (windowed, there, _), size in zip(kinds, sizes):
             there = there(position)
             if windowed:
                 wide = size // COLS
@@ -123,7 +132,7 @@
         return pl.ds(head * HD, HD)
 
     def scores_of(head):
-        keys = jnp.concatenate([key_ref[:, column(head)] for key_ref, _ in sources], axis=0)
+        keys = jnp.concatenate([source[0][:, column(head)] for source in sources], axis=0)
         keys = jnp.concatenate([keys, class_ref[...]], axis=1)
         query = jnp.concatenate([q_ref[:, column(head)], bias_ref[...]], axis=1)
         scores = lax.dot_general(
@@ -133,8 +142,11 @@
 
     for head in range(together):
         start = 0
-        for (_, value_ref), size in zip(sources, sizes):
-            turned_ref[head, pl.ds(0, HD), pl.ds(start, size)] = value_ref[:, column(head)].T
+        for source, (_, _, instead), size in zip(sources, kinds, sizes):
+            value = source[1][:, column(head)]
+            if instead is not None:
+                value = jnp.where(instead(position), source[2][:, column(head)], value)
+            turned_ref[head, pl.ds(0, HD), pl.ds(start, size)] = value.T
             start += size
     upcoming = scores_of(0)
     for head in range(together):
@@ -159,37 +171,44 @@
             stat_out[8 * head + 1 : 8 * head + 2, :] = norm
 
 
-def attend(window, query, sources, state, last):
+def attend(window, query, sources, state, last, part=None):
     tokens, width = query.shape
-    heads = width // HD
-    together = next(n for n in (3, 2, 1) if heads % n == 0)
-    kinds = tuple(source[4:] for source in sources)
+    first_head, heads = part or (0, width // HD)
+    together = next(n for n in (3, 2, 1) if heads % n == 0 and first_head % n == 0)
+    kinds = tuple((*source[4:6], source[7] if source[6:] else None) for source in sources)
 
     def columns(rows, base):
         return pl.BlockSpec((rows, HD * together), lambda h, window: (0, base // together + h))
 
-    specs, operands = [columns(tokens, 0)], [query]
+    specs, operands = [columns(tokens, first_head)], [query]
     keys_count = 0
-    for key, key_base, value, value_base, _, _ in sources:
+    for key, key_base, value, value_base, _, _, *other in sources:
         specs += [columns(key.shape[0], key_base), columns(key.shape[0], value_base)]
         operands += [key, value]
+        if other:
+            specs.append(columns(key.shape[0], value_base))
+            operands.append(other[0])
         keys_count += key.shape[0]
+    base = first_head // together
     state_specs = [
-        pl.BlockSpec((HD * together, tokens), lambda h, window: (h, 0)),
-        pl.BlockSpec((8 * together, tokens), lambda h, window: (h, 0)),
+        pl.BlockSpec((HD * together, tokens), lambda h, window: (base + h, 0)),
+        pl.BlockSpec((8 * together, tokens), lambda h, window: (base + h, 0)),
     ]
-    moved_bytes = 2 * (tokens + 2 * keys_count) * width
+    moved_bytes = 2 * (tokens + 2 * keys_count) * heads * HD
+    aliases = {}
     if state is not None:
+        if not last:
+            aliases = {1 + len(operands): 0, 2 + len(operands): 1}
         specs += state_specs
         operands += list(state)
-        moved_bytes += 4 * tokens * width
+        moved_bytes += 4 * tokens * heads * HD
     if last:
         out_shape = jax.ShapeDtypeStruct((tokens, width), jnp.bfloat16)
-        out_specs = columns(tokens, 0)
+        out_specs = columns(tokens, first_head)
     else:
         out_shape = [
             jax.ShapeDtypeStruct((width, tokens), jnp.float32),
-            jax.ShapeDtypeStruct((8 * heads, tokens), jnp.float32),
+            jax.ShapeDtypeStruct((width // HD * 8, tokens), jnp.float32),
         ]
         out_specs = state_specs
     return pl.pallas_call(
@@ -206,10 +225,11 @@
                 pltpu.VMEM((together, HD + ONES, keys_count), jnp.bfloat16),
             ],
         ),
+        input_output_aliases=aliases,
         compiler_params=pltpu.CompilerParams(vmem_limit_bytes=67_043_328),
         cost_estimate=pl.CostEstimate(
-            flops=4 * tokens * keys_count * width,
-            bytes_accessed=moved_bytes + 2 * tokens * width,
+            flops=4 * tokens * keys_count * heads * HD,
+            bytes_accessed=moved_bytes + 2 * tokens * heads * HD,
             transcendentals=tokens * keys_count * heads,
         ),
     )(window, *operands)
@@ -230,9 +250,23 @@
 
     outward = [(1, is_odd), (-1, is_even)]
     inward = [(1, is_even), (-1, is_odd)]
+    hop = [(-2, lambda f: f % 4 == 3 and f + 1 < frames), (2, lambda f: f % 4 == 0 and f > 0)]
+    skip = [(3, lambda f: f % 4 == 1), (-3, lambda f: f % 4 == 2)]
+
+    def turning(position):
+        return (position + 1) % 4 < 2
+
     beyond_keys = moved(keys, outward)
-    beyond_values = moved(values, outward)
-    beyond = [beyond_keys, beyond_values]
+    half = heads // 2
+    halves = [(0, half), (half, heads - half)]
+    beyond_values = []
+    for which, (start, number) in enumerate(halves):
+        columns = values[:, start * HD : (start + number) * HD]
+        steps = outward
+        if shared and which == 1:
+            around = moved(columns, hop)
+            steps = [(1, lambda f: f % 4 == 1), (-1, lambda f: f % 4 == 2)]
+        beyond_values.append(moved(columns, steps))
 
     far = []
     for column in sorted(range(len(offsets)), key=lambda c: -abs(offsets[c])):
@@ -262,9 +296,9 @@
     if shared:
         back, ahead = offsets.index(-2), offsets.index(2)
 
-        def two_on(position):
+        def past(position):
             odd = position % 2
-            return position + 2 - 4 * odd, jnp.where(odd == 0, back, ahead)
+            return position - 1 + 2 * odd, jnp.where(odd == 0, ahead, back)
 
         def two_back(position):
             return there(position - 2 + 4 * (position % 2))
@@ -273,34 +307,49 @@
             odd = position % 2
             return position + 1 - 2 * odd, jnp.where(odd == 0, back, ahead)
 
-        far.append(([(2, is_even), (-2, is_odd)], two_on, two_back))
-    blocks = gather(far_picks, keys, values, [reader for _, reader, _ in far], frames)
+    blocks = gather(far_picks, [keys, values], [reader for _, reader, _ in far], frames)
     arrived = []
     for block, (steps, _, _) in zip(blocks, far):
         arrived.append(moved(block, steps))
     mate_keys = moved(keys, inward)
     mate_values = moved(values, inward)
 
+    if shared:
+        (behind,) = gather(far_picks, [mate_keys, mate_values], [past], frames)
+        behind = moved(behind, outward)
+        around = moved(around, skip)
+
     def always(position):
         return position >= 0
 
     def near_there(position):
         return there(beyond_of(position))
 
+    def ahead_there(position):
+        return there(position + 2 - 4 * (position % 2))
+
     own = [(keys, 0, values, 0, True, always), (mate_keys, 0, mate_values, 0, True, always)]
     state = attend(win_rows, query, own, None, False)
-    nearby = [(beyond[0], 0, beyond[1], 0, True, near_there)]
-    if shared:
-        (handed,) = gather(far_picks, *beyond, [partner], frames)
-        handed = moved(handed, inward)
-        nearby.append(
-            (handed, 0, handed, heads, False, lambda p: there(p + 2 - 4 * (p % 2)))
-        )
-    state = attend(win_rows, query, nearby, state, False)
     distant = [
         (block, 0, block, heads, False, there) for block, (_, _, there) in zip(arrived, far)
     ]
-    return attend(win_rows, query, distant, state, True)[None]
+    if shared:
+        state = attend(win_rows, query, distant, state, False)
+    for which, part in enumerate(halves):
+        nearby = [(beyond_keys, part[0], beyond_values[which], 0, True, near_there)]
+        if shared and which == 1:
+            nearby = [(*nearby[0], around, turning)]
+        state = attend(win_rows, query, nearby, state, False, part)
+    if not shared:
+        return attend(win_rows, query, distant, state, True)[None]
+    whole = [beyond_keys, *beyond_values, around]
+    (handed,) = gather(far_picks, whole, [partner], frames, turning)
+    handed = moved(handed, inward)
+    rest = [
+        (handed, 0, handed, heads, False, ahead_there),
+        (behind, 0, behind, heads, False, two_back),
+    ]
+    return attend(win_rows, query, rest, state, True)[None]
 
 
 def solution(mesh):

time: 152 us -> 152 us (level)
  the two profiles are of different devices: /device:TPU:18 before, /device:TPU:1 now
where the time goes in v3:
time: 152 us; the launch traced here: 151 us
  waiting for transfers between devices  56.5 us (37%)
  Pallas kernels  47.9 us (32%)
  starting transfers between devices  43.6 us (29%)
  local copies, waits for them, and re-layouts  2.35 us (2%)
    ppermute x12, waiting for transfers between devices, moved(): return lax.ppermute(value, 'frame', pairs)  56.5 us
    ppermute x12, starting transfers between devices, moved(): return lax.ppermute(value, 'frame', pairs)  43.6 us
    pallas_call x5, Pallas kernels, attend(): pl.pallas_call(functools.partial(attend_kernel, kinds, together, state is...  38.6 us
    pallas_call x3, Pallas kernels, gather(): pl.pallas_call(functools.partial(gather_kernel, readers, frames, len(arra...  9.33 us
  transfers between devices with their start and end apart: 12, of which 3 were waited for; matrix products, arithmetic and copies ran while one was open for 0% of the time, Pallas kernels for 27%

profile of v3, /device:TPU:1, one launch (start us, length us, event | category | flops | bytes accessed | tf_op | source)
XLA Modules:
  0.0 151.2 jit_solution(4662310811152287285)
XLA Ops:
  0.0 2.4 %fusion = (bf16[512,768]{1,0:T(8,128)(2,1)}, bf16[512,768]{1,0:T(8,128)(2,1)S(1)}) fusion(bf16[512,1536]{1,0:T(8,128)(2,1)} %bitcast.3.refs_1_), kind=kLoop, calls=%fused_computation | loop fusion | bytes 3145728 | tf_op jit(solution)/shard_map/slice | solution.py:264
  2.4 4.5 %collective-permute-start.1 = (bf16[512,768]{1,0:T(8,128)(2,1)S(1)}, bf16[512,768]{1,0:T(8,128)(2,1)}, u32[]{:S(2)}, u32[]{:S(2)}) collective-permute-start(bf16[512,768]{1,0:T(8,128)(2,1)S(1)} %get-tuple-element.28), channel_id=1, source_target_pairs={{1,2},{3,4},{5,6},{7,8},{9,10},{11,12},{13,14},{2,1},{4,3},{6,5},{... | collective-permute-start | bytes 2359304 | tf_op jit(solution)/shard_map/ppermute | solution.py:29
  6.9 1.9 %collective-permute-start = (bf16[512,1536]{1,0:T(8,128)(2,1)}, bf16[512,1536]{1,0:T(8,128)(2,1)}, u32[]{:S(2)}, u32[]{:S(2)}) collective-permute-start(bf16[512,1536]{1,0:T(8,128)(2,1)} %bitcast.2.refs_0_), channel_id=1, source_target_pairs={{1,2},{3,4},{5,6},{7,8},{9,10},{11,12},{13,14},{2,1},{4,3},{6,5},{... | collective-permute-start | bytes 4718600 | tf_op jit(solution)/shard_map/ppermute | solution.py:29
  8.8 1.3 collective-permute-start.3
  10.1 0.1 collective-permute-start.6
  10.2 0.5 collective-permute-start.7
  10.7 30.4 %collective-permute-done.1.refs_1_ = bf16[512,768]{1,0:T(8,128)(2,1)} collective-permute-done((bf16[512,768]{1,0:T(8,128)(2,1)S(1)}, bf16[512,768]{1,0:T(8,128)(2,1)}, u32[]{:S(2)}, u32[]{:S(2)}) %collective-permute-start.1) | collective-permute-done | bytes 786464 | tf_op jit(solution)/shard_map/ppermute | solution.py:29
  41.1 4.5 %collective-permute-start.2 = (bf16[512,768]{1,0:T(8,128)(2,1)}, bf16[512,768]{1,0:T(8,128)(2,1)}, u32[]{:S(2)}, u32[]{:S(2)}) collective-permute-start(bf16[512,768]{1,0:T(8,128)(2,1)} %get-tuple-element.27), channel_id=1, source_target_pairs={{1,2},{5,6},{9,10},{13,14},{2,1},{6,5},{10,9},{14,13},{17,18},{21,... | collective-permute-start | bytes 2359304 | tf_op jit(solution)/shard_map/ppermute | solution.py:29
  45.6 0.0 collective-permute-done.3
  45.6 9.5 %collective-permute-start.4 = (bf16[512,768]{1,0:T(8,128)(2,1)}, bf16[512,768]{1,0:T(8,128)(2,1)}, u32[]{:S(2)}, u32[]{:S(2)}) collective-permute-start(bf16[512,768]{1,0:T(8,128)(2,1)} %collective-permute-done.3), channel_id=1, source_target_pairs={{1,4},{5,8},{9,12},{6,3},{10,7},{14,11},{17,20},{21,24},{25,28},{2... | collective-permute-start | bytes 2359304 | tf_op jit(solution)/shard_map/ppermute | solution.py:29
  55.0 3.8 %shard_map.57 = (bf16[128,3072]{1,0:T(8,128)(2,1)}, bf16[128,3072]{1,0:T(8,128)(2,1)}, bf16[128,3072]{1,0:T(8,128)(2,1)}) custom-call(s32[6,16]{1,0:T(8,128)} %bitcast.10, bf16[512,1536]{1,0:T(8,128)(2,1)} %bitcast.2.refs_0_, bf16[512,1536]{1,0:T(8,128)(2,1)} %bitcast.3.refs_1_), custom_call_target="tpu_custom_call" | custom-call | bytes 4718592 | tf_op jit(solution)/shard_map/pallas_call | solution.py:75
  58.8 7.7 %collective-permute-done.2.refs_2_.refs_1_ = bf16[512,768]{1,0:T(8,128)(2,1)} collective-permute-done((bf16[512,768]{1,0:T(8,128)(2,1)}, bf16[512,768]{1,0:T(8,128)(2,1)}, u32[]{:S(2)}, u32[]{:S(2)}) %collective-permute-start.2) | collective-permute-done | bytes 786464 | tf_op jit(solution)/shard_map/ppermute | solution.py:29
  66.5 13.6 %collective-permute-start.10 = (bf16[128,3072]{1,0:T(8,128)(2,1)}, bf16[128,3072]{1,0:T(8,128)(2,1)}, u32[]{:S(2)}, u32[]{:S(2)}) collective-permute-start(bf16[128,3072]{1,0:T(8,128)(2,1)} %get-tuple-element.17), channel_id=1, source_target_pairs={{0,4},{1,5},{2,6},{3,7},{4,8},{5,9},{6,10},{7,11},{8,12},{9,13},{1... | collective-permute-start | bytes 2359304 | tf_op jit(solution)/shard_map/ppermute | solution.py:29
  80.1 0.0 collective-permute-done.refs_0_
  80.1 1.3 collective-permute-start.11
  81.4 0.0 collective-permute-done.4.refs_3_.refs_2_
  81.4 2.2 %collective-permute-start.9 = (bf16[128,3072]{1,0:T(8,128)(2,1)}, bf16[128,3072]{1,0:T(8,128)(2,1)}, u32[]{:S(2)}, u32[]{:S(2)}) collective-permute-start(bf16[128,3072]{1,0:T(8,128)(2,1)} %get-tuple-element.16), channel_id=1, source_target_pairs={{0,8},{1,9},{2,10},{3,11},{4,12},{5,13},{6,14},{7,15},{8,0},{9,1},... | collective-permute-start | bytes 2359304 | tf_op jit(solution)/shard_map/ppermute | solution.py:29
  83.6 2.8 %shard_map.55 = bf16[128,3072]{1,0:T(8,128)(2,1)} custom-call(s32[6,16]{1,0:T(8,128)} %bitcast.11, bf16[512,1536]{1,0:T(8,128)(2,1)} %collective-permute-done.refs_0_, bf16[512,768]{1,0:T(8,128)(2,1)} %collective-permute-done.1.refs_1_, bf16[512,768]{1,0:T(8,128)(2,1)} %collective-permute-done.2.refs_2_.refs_1_, ...), custom_call_target="tpu_custom_call" | custom-call | bytes 1572864 | tf_op jit(solution)/shard_map/pallas_call | solution.py:75
  86.4 0.0 collective-permute-done.6.refs_0_.refs_2_
  86.4 0.1 collective-permute-start.5
  86.5 0.0 collective-permute-done.7.refs_1_.refs_3_
  86.5 2.8 %shard_map.56 = bf16[128,3072]{1,0:T(8,128)(2,1)} custom-call(s32[6,16]{1,0:T(8,128)} %bitcast.12, bf16[512,1536]{1,0:T(8,128)(2,1)} %collective-permute-done.6.refs_0_.refs_2_, bf16[512,1536]{1,0:T(8,128)(2,1)} %collective-permute-done.7.refs_1_.refs_3_), custom_call_target="tpu_custom_call" | custom-call | bytes 1572864 | tf_op jit(solution)/shard_map/pallas_call | solution.py:75
  89.3 4.2 %collective-permute-start.8 = (bf16[128,3072]{1,0:T(8,128)(2,1)}, bf16[128,3072]{1,0:T(8,128)(2,1)}, u32[]{:S(2)}, u32[]{:S(2)}) collective-permute-start(bf16[128,3072]{1,0:T(8,128)(2,1)} %shard_map.56), channel_id=1, source_target_pairs={{1,2},{3,4},{5,6},{7,8},{9,10},{11,12},{13,14},{2,1},{4,3},{6,5},{... | collective-permute-start | bytes 2359304 | tf_op jit(solution)/shard_map/ppermute | solution.py:29
  94.1 12.2 %shard_map.58 = (f32[1536,512]{1,0:T(8,128)}, f32[96,512]{1,0:T(8,128)}) custom-call(s32[1]{0:T(128)S(6)} %copy.18.window_ref, bf16[512,1536]{1,0:T(8,128)(2,1)} %bitcast.5, bf16[512,1536]{1,0:T(8,128)(2,1)} %bitcast.2.refs_0_, bf16[512,1536]{1,0:T(8,128)(2,1)} %bitcast.3.refs_1_, bf16[512,1536]{1,0:T(8,128)(2,1)} %collective-permute-done.6.refs_0_.refs_2_, ...), custom_call_target="tpu_custom_call" | custom-call | flops 3221225472 | bytes 9437184 | tf_op jit(solution)/shard_map/pallas_call | solution.py:214
  106.3 0.0 collective-permute-done.10.refs_2_.refs_3_
  106.3 0.0 collective-permute-done.11.refs_4_.refs_5_
  106.3 18.4 %collective-permute-done.9.refs_0_.refs_1_ = bf16[128,3072]{1,0:T(8,128)(2,1)} collective-permute-done((bf16[128,3072]{1,0:T(8,128)(2,1)}, bf16[128,3072]{1,0:T(8,128)(2,1)}, u32[]{:S(2)}, u32[]{:S(2)}) %collective-permute-start.9) | collective-permute-done | bytes 786464 | tf_op jit(solution)/shard_map/ppermute | solution.py:29
  124.8 8.1 %shard_map.59 = (f32[1536,512]{1,0:T(8,128)}, f32[96,512]{1,0:T(8,128)}) custom-call(s32[1]{0:T(128)S(6)} %copy.18.window_ref, bf16[512,1536]{1,0:T(8,128)(2,1)} %bitcast.6, bf16[128,3072]{1,0:T(8,128)(2,1)} %collective-permute-done.9.refs_0_.refs_1_, ...), custom_call_target="tpu_custom_call", output_to_operand_aliasing={{0}: (8, {}), {1}: (9, {})} | custom-call | flops 1207959552 | bytes 8650752 | tf_op jit(solution)/shard_map/pallas_call | solution.py:214
  132.8 5.5 %shard_map.60 = (f32[1536,512]{1,0:T(8,128)}, f32[96,512]{1,0:T(8,128)}) custom-call(s32[1]{0:T(128)S(6)} %copy.18.window_ref, bf16[512,1536]{1,0:T(8,128)(2,1)} %bitcast.7, bf16[512,1536]{1,0:T(8,128)(2,1)} %collective-permute-done.refs_0_, bf16[512,768]{1,0:T(8,128)(2,1)} %collective-permute-done.1.refs_1_, ...), custom_call_target="tpu_custom_call", output_to_operand_aliasing={{0}: (4, {}), {1}: (5, {})} | custom-call | flops 805306368 | bytes 4718592 | tf_op jit(solution)/shard_map/pallas_call | solution.py:214
  138.3 5.7 %shard_map.61 = (f32[1536,512]{1,0:T(8,128)}, f32[96,512]{1,0:T(8,128)}) custom-call(s32[1]{0:T(128)S(6)} %copy.18.window_ref, bf16[512,1536]{1,0:T(8,128)(2,1)} %bitcast.8, bf16[512,1536]{1,0:T(8,128)(2,1)} %collective-permute-done.refs_0_, bf16[512,768]{1,0:T(8,128)(2,1)} %collective-permute-done.2.refs_2_.refs_1_, ...), custom_call_target="tpu_custom_call", output_to_operand_aliasing={{0}: (5, {}), {1}: (6, {})} | custom-call | flops 805306368 | bytes 4718592 | tf_op jit(solution)/shard_map/pallas_call | solution.py:214
  144.1 0.0 collective-permute-done.5.refs_0_.refs_1_
  144.1 0.0 collective-permute-done.8.refs_2_.refs_3_
  144.1 7.1 %shard_map.62 = bf16[512,1536]{1,0:T(8,128)(2,1)} custom-call(s32[1]{0:T(128)S(6)} %copy.18.window_ref, bf16[512,1536]{1,0:T(8,128)(2,1)} %bitcast.9, bf16[128,3072]{1,0:T(8,128)(2,1)} %collective-permute-done.5.refs_0_.refs_1_, bf16[128,3072]{1,0:T(8,128)(2,1)} %collective-permute-done.5.refs_0_.refs_1_, ...), custom_call_target="tpu_custom_call" | custom-call | flops 805306368 | bytes 7864320 | tf_op jit(solution)/shard_map/pallas_call | solution.py:214
Async XLA Ops:
  2.4 38.7 %collective-permute-start.1 = (bf16[512,768]{1,0:T(8,128)(2,1)S(1)}, bf16[512,768]{1,0:T(8,128)(2,1)}, u32[]{:S(2)}, u32[]{:S(2)}) collective-permute-start(bf16[512,768]{1,0:T(8,128)(2,1)S(1)} %get-tuple-element.28), channel_id=1, source_target_pairs={{1,2},{3,4},{5,6},{7,8},{9,10},{11,12},{13,14},{2,1},{4,3},{6,5},{... | collective-permute-start | bytes 2359304 | tf_op jit(solution)/shard_map/ppermute | solution.py:29
  6.9 73.2 %collective-permute-start = (bf16[512,1536]{1,0:T(8,128)(2,1)}, bf16[512,1536]{1,0:T(8,128)(2,1)}, u32[]{:S(2)}, u32[]{:S(2)}) collective-permute-start(bf16[512,1536]{1,0:T(8,128)(2,1)} %bitcast.2.refs_0_), channel_id=1, source_target_pairs={{1,2},{3,4},{5,6},{7,8},{9,10},{11,12},{13,14},{2,1},{4,3},{6,5},{... | collective-permute-start | bytes 4718600 | tf_op jit(solution)/shard_map/ppermute | solution.py:29
  8.8 36.8 %collective-permute-start.3 = (bf16[512,768]{1,0:T(8,128)(2,1)}, bf16[512,768]{1,0:T(8,128)(2,1)}, u32[]{:S(2)}, u32[]{:S(2)}) collective-permute-start(bf16[512,768]{1,0:T(8,128)(2,1)} %get-tuple-element.27), channel_id=1, source_target_pairs={{3,1},{7,5},{11,9},{4,6},{8,10},{12,14},{19,17},{23,21},{27,25},{2... | collective-permute-start | bytes 2359304 | tf_op jit(solution)/shard_map/ppermute | solution.py:29
  10.1 76.3 %collective-permute-start.6 = (bf16[512,1536]{1,0:T(8,128)(2,1)}, bf16[512,1536]{1,0:T(8,128)(2,1)}, u32[]{:S(2)}, u32[]{:S(2)}) collective-permute-start(bf16[512,1536]{1,0:T(8,128)(2,1)} %bitcast.2.refs_0_), channel_id=1, source_target_pairs={{0,1},{2,3},{4,5},{6,7},{8,9},{10,11},{12,13},{14,15},{1,0},{3,2},... | collective-permute-start | bytes 4718600 | tf_op jit(solution)/shard_map/ppermute | solution.py:29
  10.2 76.3 %collective-permute-start.7 = (bf16[512,1536]{1,0:T(8,128)(2,1)}, bf16[512,1536]{1,0:T(8,128)(2,1)}, u32[]{:S(2)}, u32[]{:S(2)}) collective-permute-start(bf16[512,1536]{1,0:T(8,128)(2,1)} %bitcast.3.refs_1_), channel_id=1, source_target_pairs={{0,1},{2,3},{4,5},{6,7},{8,9},{10,11},{12,13},{14,15},{1,0},{3,2},... | collective-permute-start | bytes 4718600 | tf_op jit(solution)/shard_map/ppermute | solution.py:29
  41.1 25.4 %collective-permute-start.2 = (bf16[512,768]{1,0:T(8,128)(2,1)}, bf16[512,768]{1,0:T(8,128)(2,1)}, u32[]{:S(2)}, u32[]{:S(2)}) collective-permute-start(bf16[512,768]{1,0:T(8,128)(2,1)} %get-tuple-element.27), channel_id=1, source_target_pairs={{1,2},{5,6},{9,10},{13,14},{2,1},{6,5},{10,9},{14,13},{17,18},{21,... | collective-permute-start | bytes 2359304 | tf_op jit(solution)/shard_map/ppermute | solution.py:29
  45.6 35.8 %collective-permute-start.4 = (bf16[512,768]{1,0:T(8,128)(2,1)}, bf16[512,768]{1,0:T(8,128)(2,1)}, u32[]{:S(2)}, u32[]{:S(2)}) collective-permute-start(bf16[512,768]{1,0:T(8,128)(2,1)} %collective-permute-done.3), channel_id=1, source_target_pairs={{1,4},{5,8},{9,12},{6,3},{10,7},{14,11},{17,20},{21,24},{25,28},{2... | collective-permute-start | bytes 2359304 | tf_op jit(solution)/shard_map/ppermute | solution.py:29
  66.5 39.9 %collective-permute-start.10 = (bf16[128,3072]{1,0:T(8,128)(2,1)}, bf16[128,3072]{1,0:T(8,128)(2,1)}, u32[]{:S(2)}, u32[]{:S(2)}) collective-permute-start(bf16[128,3072]{1,0:T(8,128)(2,1)} %get-tuple-element.17), channel_id=1, source_target_pairs={{0,4},{1,5},{2,6},{3,7},{4,8},{5,9},{6,10},{7,11},{8,12},{9,13},{1... | collective-permute-start | bytes 2359304 | tf_op jit(solution)/shard_map/ppermute | solution.py:29
  80.1 26.2 %collective-permute-start.11 = (bf16[128,3072]{1,0:T(8,128)(2,1)}, bf16[128,3072]{1,0:T(8,128)(2,1)}, u32[]{:S(2)}, u32[]{:S(2)}) collective-permute-start(bf16[128,3072]{1,0:T(8,128)(2,1)} %get-tuple-element.18), channel_id=1, source_target_pairs={{4,0},{5,1},{6,2},{7,3},{8,4},{9,5},{10,6},{11,7},{12,8},{13,9},{1... | collective-permute-start | bytes 2359304 | tf_op jit(solution)/shard_map/ppermute | solution.py:29
  81.4 43.4 %collective-permute-start.9 = (bf16[128,3072]{1,0:T(8,128)(2,1)}, bf16[128,3072]{1,0:T(8,128)(2,1)}, u32[]{:S(2)}, u32[]{:S(2)}) collective-permute-start(bf16[128,3072]{1,0:T(8,128)(2,1)} %get-tuple-element.16), channel_id=1, source_target_pairs={{0,8},{1,9},{2,10},{3,11},{4,12},{5,13},{6,14},{7,15},{8,0},{9,1},... | collective-permute-start | bytes 2359304 | tf_op jit(solution)/shard_map/ppermute | solution.py:29
  86.4 57.7 %collective-permute-start.5 = (bf16[128,3072]{1,0:T(8,128)(2,1)}, bf16[128,3072]{1,0:T(8,128)(2,1)}, u32[]{:S(2)}, u32[]{:S(2)}) collective-permute-start(bf16[128,3072]{1,0:T(8,128)(2,1)} %shard_map.55), channel_id=1, source_target_pairs={{0,1},{2,3},{4,5},{6,7},{8,9},{10,11},{12,13},{14,15},{1,0},{3,2},... | collective-permute-start | bytes 2359304 | tf_op jit(solution)/shard_map/ppermute | solution.py:29
  89.3 54.8 %collective-permute-start.8 = (bf16[128,3072]{1,0:T(8,128)(2,1)}, bf16[128,3072]{1,0:T(8,128)(2,1)}, u32[]{:S(2)}, u32[]{:S(2)}) collective-permute-start(bf16[128,3072]{1,0:T(8,128)(2,1)} %shard_map.56), channel_id=1, source_target_pairs={{1,2},{3,4},{5,6},{7,8},{9,10},{11,12},{13,14},{2,1},{4,3},{6,5},{... | collective-permute-start | bytes 2359304 | tf_op jit(solution)/shard_map/ppermute | solution.py:29

commit v4 on v3

--- a/solution.py
+++ b/solution.py
@@ -41,68 +41,86 @@
     return frame % 2 == 1
 
 
-def gather_kernel(readers, frames, count, instead, picks_ref, *refs):
-    arrays, outs = refs[:count], refs[count : count + len(readers)]
-    sems = refs[count + len(readers)]
+def gather_kernel(readers, frames, count, parts, picks_ref, *refs):
+    arrays, outs = refs[:count], refs[count:-1]
+    sems = refs[-1]
     position = lax.axis_index("frame")
-
-    def copy_all(arrays):
-        copies = []
-        for slot, (reader_of, out) in enumerate(zip(readers, outs)):
-            reader, column = reader_of(position)
-            pick = picks_ref[column, jnp.clip(reader, 0, frames - 1)]
-            rows = pl.ds(pl.multiple_of(pick * SUB, SUB), SUB)
-            start = 0
-            for which, source in enumerate(arrays):
-                target = out.at[:, pl.ds(start, source.shape[1])]
-                sem = sems.at[count * slot + which]
-                copies.append(pltpu.make_async_copy(source.at[rows, :], target, sem))
-                start += source.shape[1]
-        for copy in copies:
-            copy.start()
-        for copy in copies:
-            copy.wait()
-
-    if instead is None:
-        copy_all(arrays)
-    else:
-        pl.when(instead(position))(lambda: copy_all([*arrays[:-2], arrays[-1]]))
-        pl.when(jnp.logical_not(instead(position)))(lambda: copy_all(arrays[:-1]))
-
-
-def gather(picks, arrays, readers, frames, instead=None):
-    width = sum(array.shape[1] for array in (arrays if instead is None else arrays[:-1]))
+    copies = []
+
+    def copy(source, target):
+        copies.append(pltpu.make_async_copy(source, target, sems.at[len(copies)]))
+
+    def block(pick):
+        return pl.ds(pl.multiple_of(pick * SUB, SUB), SUB)
+
+    def pick_of(reader_of):
+        reader, column = reader_of(position)
+        return picks_ref[column, jnp.clip(reader, 0, frames - 1)]
+
+    for reader_of, out in zip(readers[:-1] if parts else readers, outs):
+        rows = block(pick_of(reader_of))
+        start = 0
+        for source in arrays:
+            copy(source.at[rows, :], out.at[:, pl.ds(start, source.shape[1])])
+            start += source.shape[1]
+    if parts:
+        pick, source = pick_of(readers[-1]), arrays[-1]
+        outs = outs[len(readers) - 1 :]
+        copy(source.at[block(pick), :], outs[0])
+        for (start, width), out in zip(parts, outs[1:]):
+            for other in range(source.shape[0] // SUB - 1):
+                rows = block(other + jnp.where(other >= pick, 1, 0))
+                target = out.at[pl.ds(other * SUB, SUB), :]
+                copy(source.at[rows, pl.ds(start, width)], target)
+    for each in copies:
+        each.start()
+    for each in copies:
+        each.wait()
+
+
+def gather(picks, arrays, readers, frames, parts=()):
+    width = sum(array.shape[1] for array in arrays)
+    dtype = arrays[0].dtype
+    shapes = [(SUB, width)] * (len(readers) - bool(parts))
+    count = len(shapes) * len(arrays)
+    if parts:
+        tokens, last_width = arrays[-1].shape
+        shapes += [(SUB, last_width)] + [(tokens - SUB, width) for _, width in parts]
+        count += 1 + (tokens // SUB - 1) * len(parts)
     return pl.pallas_call(
-        functools.partial(gather_kernel, readers, frames, len(arrays), instead),
-        out_shape=[jax.ShapeDtypeStruct((SUB, width), arrays[0].dtype) for _ in readers],
+        functools.partial(gather_kernel, readers, frames, len(arrays), parts),
+        out_shape=[jax.ShapeDtypeStruct(shape, dtype) for shape in shapes],
         in_specs=[
             pl.BlockSpec(memory_space=pltpu.SMEM),
             *[pl.BlockSpec(memory_space=pltpu.HBM)] * len(arrays),
         ],
-        out_specs=[pl.BlockSpec(memory_space=pltpu.VMEM) for _ in readers],
-        scratch_shapes=[pltpu.SemaphoreType.DMA((len(arrays) * len(readers),))],
+        out_specs=[pl.BlockSpec(memory_space=pltpu.VMEM) for _ in shapes],
+        scratch_shapes=[pltpu.SemaphoreType.DMA((count,))],
         compiler_params=pltpu.CompilerParams(vmem_limit_bytes=67_043_328),
         cost_estimate=pl.CostEstimate(
-            flops=0, bytes_accessed=4 * SUB * width * len(readers), transcendentals=0
+            flops=0,
+            bytes_accessed=4 * sum(rows * columns for rows, columns in shapes),
+            transcendentals=0,
         ),
     )(picks.T, *arrays)
 
 
-def attend_kernel(kinds, together, first, last, window_ref, q_ref, *refs):
+def attend_kernel(kinds, together, first, last, onto, window_ref, picks_ref, q_ref, *refs):
     sources = []
-    for _, _, instead in kinds:
-        count = 2 if instead is None else 3
-        sources.append(refs[:count])
-        refs = refs[count:]
+    for count, *_ in kinds:
+        sources.append((refs[0], refs[1 : 1 + count]))
+        refs = refs[1 + count :]
     if not first:
         acc_in, stat_in = refs[:2]
         refs = refs[2:]
+    if onto:
+        refs = refs[1:]
     if last:
         out_ref, bias_ref, class_ref, turned_ref = refs
     else:
         acc_out, stat_out, bias_ref, class_ref, turned_ref = refs
     tokens = q_ref.shape[0]
-    sizes = [source[0].shape[0] for source in sources]
+    sizes = [key_ref.shape[0] for key_ref, _ in sources]
     position = lax.axis_index("frame")
 
     @pl.when(pl.program_id(0) == 0)
@@ -111,7 +129,7 @@
         lane = lax.broadcasted_iota(jnp.int32, (tokens, HD), 1)
         bias = jnp.zeros((tokens, HD), jnp.float32)
         base, start = 0, 0
-        for (windowed, there, _), size in zip(kinds, sizes):
+        for (_, windowed, there, _), size in zip(kinds, sizes):
             there = there(position)
             if windowed:
                 wide = size // COLS
@@ -132,7 +150,7 @@
         return pl.ds(head * HD, HD)
 
     def scores_of(head):
-        keys = jnp.concatenate([source[0][:, column(head)] for source in sources], axis=0)
+        keys = jnp.concatenate([key_ref[:, column(head)] for key_ref, _ in sources], axis=0)
         keys = jnp.concatenate([keys, class_ref[...]], axis=1)
         query = jnp.concatenate([q_ref[:, column(head)], bias_ref[...]], axis=1)
         scores = lax.dot_general(
@@ -142,11 +160,25 @@
 
     for head in range(together):
         start = 0
-        for source, (_, _, instead), size in zip(sources, kinds, sizes):
-            value = source[1][:, column(head)]
-            if instead is not None:
-                value = jnp.where(instead(position), source[2][:, column(head)], value)
-            turned_ref[head, pl.ds(0, HD), pl.ds(start, size)] = value.T
+        for (_, value_refs), (*_, parted), size in zip(sources, kinds, sizes):
+
+            def put(value, start):
+                turned_ref[head, pl.ds(0, HD), pl.ds(start, value.shape[0])] = value.T
+
+            if parted is None:
+                put(value_refs[0][:, column(head)], start)
+            else:
+                reader_of, choose = parted
+                reader, which = reader_of(position)
+                pick = picks_ref[which, jnp.clip(reader, 0, picks_ref.shape[1] - 1)]
+                others = value_refs[1][:, column(head)]
+                if value_refs[2:]:
+                    others = jnp.where(choose(position), value_refs[2][:, column(head)], others)
+                put(value_refs[0][:, column(head)], pl.multiple_of(start + pick * SUB, SUB))
+                for other in range(size // SUB - 1):
+                    block = other + jnp.where(other >= pick, 1, 0)
+                    part = others[other * SUB : (other + 1) * SUB]
+                    put(part, pl.multiple_of(start + block * SUB, SUB))
             start += size
     upcoming = scores_of(0)
     for head in range(together):
@@ -171,23 +203,22 @@
             stat_out[8 * head + 1 : 8 * head + 2, :] = norm
 
 
-def attend(window, query, sources, state, last, part=None):
+def attend(window, picks, query, sources, state, last, part=None, target=None):
     tokens, width = query.shape
     first_head, heads = part or (0, width // HD)
     together = next(n for n in (3, 2, 1) if heads % n == 0 and first_head % n == 0)
-    kinds = tuple((*source[4:6], source[7] if source[6:] else None) for source in sources)
+    kinds = tuple((len(source[2]), *source[4:]) for source in sources)
 
     def columns(rows, base):
         return pl.BlockSpec((rows, HD * together), lambda h, window: (0, base // together + h))
 
-    specs, operands = [columns(tokens, first_head)], [query]
+    specs = [pl.BlockSpec(memory_space=pltpu.SMEM), columns(tokens, first_head)]
+    operands = [picks.T, query]
     keys_count = 0
-    for key, key_base, value, value_base, _, _, *other in sources:
-        specs += [columns(key.shape[0], key_base), columns(key.shape[0], value_base)]
-        operands += [key, value]
-        if other:
-            specs.append(columns(key.shape[0], value_base))
-            operands.append(other[0])
+    for key, key_base, values, value_bases, *_ in sources:
+        specs.append(columns(key.shape[0], key_base))
+        specs += [columns(value.shape[0], base) for value, base in zip(values, value_bases)]
+        operands += [key, *values]
         keys_count += key.shape[0]
     base = first_head // together
     state_specs = [
@@ -202,6 +233,10 @@
         specs += state_specs
         operands += list(state)
         moved_bytes += 4 * tokens * heads * HD
+    if target is not None:
+        aliases = {1 + len(operands): 0}
+        specs.append(pl.BlockSpec(memory_space=pl.ANY))
+        operands.append(target)
     if last:
         out_shape = jax.ShapeDtypeStruct((tokens, width), jnp.bfloat16)
         out_specs = columns(tokens, first_head)
@@ -212,7 +247,9 @@
         ]
         out_specs = state_specs
     return pl.pallas_call(
-        functools.partial(attend_kernel, kinds, together, state is None, last),
+        functools.partial(
+            attend_kernel, kinds, together, state is None, last, target is not None
+        ),
         out_shape=out_shape,
         grid_spec=pltpu.PrefetchScalarGridSpec(
             num_scalar_prefetch=1,
@@ -256,17 +293,10 @@
     def turning(position):
         return (position + 1) % 4 < 2
 
+    straight = [(1, lambda f: f % 4 == 1), (-1, lambda f: f % 4 == 2)]
     beyond_keys = moved(keys, outward)
     half = heads // 2
     halves = [(0, half), (half, heads - half)]
-    beyond_values = []
-    for which, (start, number) in enumerate(halves):
-        columns = values[:, start * HD : (start + number) * HD]
-        steps = outward
-        if shared and which == 1:
-            around = moved(columns, hop)
-            steps = [(1, lambda f: f % 4 == 1), (-1, lambda f: f % 4 == 2)]
-        beyond_values.append(moved(columns, steps))
 
     far = []
     for column in sorted(range(len(offsets)), key=lambda c: -abs(offsets[c])):
@@ -296,6 +326,10 @@
     if shared:
         back, ahead = offsets.index(-2), offsets.index(2)
 
+        def beyond_reader(position):
+            odd = position % 2
+            return position - 2 + 4 * odd, jnp.where(odd == 0, ahead, back)
+
         def past(position):
             odd = position % 2
             return position - 1 + 2 * odd, jnp.where(odd == 0, ahead, back)
@@ -307,7 +341,21 @@
             odd = position % 2
             return position + 1 - 2 * odd, jnp.where(odd == 0, back, ahead)
 
-    blocks = gather(far_picks, [keys, values], [reader for _, reader, _ in far], frames)
+    readers = [reader for _, reader, _ in far]
+    parts = [(start * HD, number * HD) for start, number in halves]
+    if shared:
+        *blocks, picked, lower, upper = gather(
+            far_picks, [keys, values], [*readers, beyond_reader], frames, tuple(parts)
+        )
+    else:
+        blocks = gather(far_picks, [keys, values], readers, frames)
+        lower, upper = [values[:, start : start + width] for start, width in parts]
+    around = []
+    if shared:
+        picked = moved(picked, outward)
+        around = [moved(lower, hop)]
+    lower = moved(lower, straight if shared else outward)
+    upper = moved(upper, outward)
     arrived = []
     for block, (steps, _, _) in zip(blocks, far):
         arrived.append(moved(block, steps))
@@ -317,7 +365,7 @@
     if shared:
         (behind,) = gather(far_picks, [mate_keys, mate_values], [past], frames)
         behind = moved(behind, outward)
-        around = moved(around, skip)
+        around = [moved(around[0], skip)]
 
     def always(position):
         return position >= 0
@@ -328,28 +376,42 @@
     def ahead_there(position):
         return there(position + 2 - 4 * (position % 2))
 
-    own = [(keys, 0, values, 0, True, always), (mate_keys, 0, mate_values, 0, True, always)]
-    state = attend(win_rows, query, own, None, False)
+    own = [
+        (keys, 0, [values], [0], True, always, None),
+        (mate_keys, 0, [mate_values], [0], True, always, None),
+    ]
+    state = attend(win_rows, far_picks, query, own, None, False)
     distant = [
-        (block, 0, block, heads, False, there) for block, (_, _, there) in zip(arrived, far)
+        (block, 0, [block], [heads], False, there, None)
+        for block, (_, _, there) in zip(arrived, far)
     ]
-    if shared:
-        state = attend(win_rows, query, distant, state, False)
-    for which, part in enumerate(halves):
-        nearby = [(beyond_keys, part[0], beyond_values[which], 0, True, near_there)]
-        if shared and which == 1:
-            nearby = [(*nearby[0], around, turning)]
-        state = attend(win_rows, query, nearby, state, False, part)
     if not shared:
-        return attend(win_rows, query, distant, state, True)[None]
-    whole = [beyond_keys, *beyond_values, around]
-    (handed,) = gather(far_picks, whole, [partner], frames, turning)
-    handed = moved(handed, inward)
-    rest = [
-        (handed, 0, handed, heads, False, ahead_there),
-        (behind, 0, behind, heads, False, two_back),
-    ]
-    return attend(win_rows, query, rest, state, True)[None]
+        for part, values in ((halves[0], lower), (halves[1], upper)):
+            nearby = [(beyond_keys, part[0], [values], [0], True, near_there, None)]
+            state = attend(win_rows, far_picks, query, nearby, state, False, part)
+        return attend(win_rows, far_picks, query, distant, state, True)[None]
+    (handed_keys,) = gather(far_picks, [beyond_keys], [partner], frames)
+    handed_values = moved(picked, inward)
+    handed_keys = moved(handed_keys, inward)
+    distant.append((handed_keys, 0, [handed_values], [0], False, ahead_there, None))
+    state = attend(win_rows, far_picks, query, distant, state, False)
+    out = None
+    for part, values in ((halves[0], [lower, *around]), (halves[1], [upper])):
+        start = part[0]
+        nearby = [
+            (
+                beyond_keys,
+                start,
+                [picked, *values],
+                [start] + [0] * len(values),
+                True,
+                near_there,
+                (partner, turning),
+            ),
+            (behind, start, [behind], [heads + start], False, two_back, None),
+        ]
+        out = attend(win_rows, far_picks, query, nearby, state, True, part, out)
+    return out[None]
 
 
 def solution(mesh):

time: 152 us -> 138 us (0.908)
  the two profiles are of different devices: /device:TPU:1 before, /device:TPU:15 now
where the time goes in v4:
time: 138 us; the launch traced here: 137 us
  starting transfers between devices  68.6 us (50%)
  Pallas kernels  44.4 us (32%)
  waiting for transfers between devices  23.1 us (17%)
    ppermute x14, starting transfers between devices, moved(): return lax.ppermute(value, 'frame', pairs)  68.6 us
    pallas_call x4, Pallas kernels, attend(): pl.pallas_call(functools.partial(attend_kernel, kinds, together, state is...  34.1 us
    ppermute x14, waiting for transfers between devices, moved(): return lax.ppermute(value, 'frame', pairs)  23.1 us
    pallas_call x3, Pallas kernels, gather(): pl.pallas_call(functools.partial(gather_kernel, readers, frames, len(arra...  10.2 us
  transfers between devices with their start and end apart: 14, of which 2 were waited for; matrix products, arithmetic and copies ran while one was open for 0% of the time, Pallas kernels for 28%

profile of v4, /device:TPU:15, one launch (start us, length us, event | category | flops | bytes accessed | tf_op | source)
XLA Modules:
  0.0 136.9 jit_solution(8707295124484028653)
XLA Ops:
  0.0 0.7 collective-permute-start.3
  0.7 0.0 collective-permute-start.4
  0.7 3.5 %collective-permute-start = (bf16[512,1536]{1,0:T(8,128)(2,1)}, bf16[512,1536]{1,0:T(8,128)(2,1)}, u32[]{:S(2)}, u32[]{:S(2)}) collective-permute-start(bf16[512,1536]{1,0:T(8,128)(2,1)} %bitcast.10), channel_id=1, source_target_pairs={{1,2},{3,4},{5,6},{7,8},{9,10},{11,12},{13,14},{2,1},{4,3},{6,5},{... | collective-permute-start | bytes 4718600 | tf_op jit(solution)/shard_map/ppermute | solution.py:29
  4.2 4.9 %shard_map.55 = (bf16[128,3072]{1,0:T(8,128)(2,1)}, bf16[128,3072]{1,0:T(8,128)(2,1)}, bf16[128,3072]{1,0:T(8,128)(2,1)}, bf16[128,1536]{1,0:T(8,128)(2,1)}, bf1...) custom-call(s32[6,16]{1,0:T(8,128)} %bitcast.16, bf16[512,1536]{1,0:T(8,128)(2,1)} %bitcast.11, bf16[512,1536]{1,0:T(8,128)(2,1)} %bitcast.14), custom_call_target="tpu_custom_call" | custom-call | bytes 7864320 | tf_op jit(solution)/shard_map/pallas_call | solution.py:90
  9.1 3.0 %collective-permute-start.12 = (bf16[384,768]{1,0:T(8,128)(2,1)}, bf16[384,768]{1,0:T(8,128)(2,1)}, u32[]{:S(2)}, u32[]{:S(2)}) collective-permute-start(bf16[384,768]{1,0:T(8,128)(2,1)} %get-tuple-element.24), channel_id=1, source_target_pairs={{3,1},{7,5},{11,9},{4,6},{8,10},{12,14},{19,17},{23,21},{27,25},{2... | collective-permute-start | bytes 1769480 | tf_op jit(solution)/shard_map/ppermute | solution.py:29
  12.1 3.5 %collective-permute-start.1 = (bf16[128,1536]{1,0:T(8,128)(2,1)}, bf16[128,1536]{1,0:T(8,128)(2,1)}, u32[]{:S(2)}, u32[]{:S(2)}) collective-permute-start(bf16[128,1536]{1,0:T(8,128)(2,1)} %get-tuple-element.15), channel_id=1, source_target_pairs={{1,2},{3,4},{5,6},{7,8},{9,10},{11,12},{13,14},{2,1},{4,3},{6,5},{... | collective-permute-start | bytes 1179656 | tf_op jit(solution)/shard_map/ppermute | solution.py:29
  15.6 12.3 %collective-permute-done.1.refs_1_ = bf16[128,1536]{1,0:T(8,128)(2,1)} collective-permute-done((bf16[128,1536]{1,0:T(8,128)(2,1)}, bf16[128,1536]{1,0:T(8,128)(2,1)}, u32[]{:S(2)}, u32[]{:S(2)}) %collective-permute-start.1) | collective-permute-done | bytes 393248 | tf_op jit(solution)/shard_map/ppermute | solution.py:29
  27.9 0.0 collective-permute-start.6
  27.9 10.8 %collective-permute-done.12 = bf16[384,768]{1,0:T(8,128)(2,1)} collective-permute-done((bf16[384,768]{1,0:T(8,128)(2,1)}, bf16[384,768]{1,0:T(8,128)(2,1)}, u32[]{:S(2)}, u32[]{:S(2)}) %collective-permute-start.12) | collective-permute-done | bytes 589856 | tf_op jit(solution)/shard_map/ppermute | solution.py:29
  38.7 3.2 %collective-permute-start.7 = (bf16[128,3072]{1,0:T(8,128)(2,1)}, bf16[128,3072]{1,0:T(8,128)(2,1)}, u32[]{:S(2)}, u32[]{:S(2)}) collective-permute-start(bf16[128,3072]{1,0:T(8,128)(2,1)} %get-tuple-element.18), channel_id=1, source_target_pairs={{0,4},{1,5},{2,6},{3,7},{4,8},{5,9},{6,10},{7,11},{8,12},{9,13},{1... | collective-permute-start | bytes 2359304 | tf_op jit(solution)/shard_map/ppermute | solution.py:29
  41.9 0.0 collective-permute-done.3.refs_0_.refs_2_
  41.9 2.9 %collective-permute-start.8 = (bf16[128,3072]{1,0:T(8,128)(2,1)}, bf16[128,3072]{1,0:T(8,128)(2,1)}, u32[]{:S(2)}, u32[]{:S(2)}) collective-permute-start(bf16[128,3072]{1,0:T(8,128)(2,1)} %get-tuple-element.19), channel_id=1, source_target_pairs={{4,0},{5,1},{6,2},{7,3},{8,4},{9,5},{10,6},{11,7},{12,8},{13,9},{1... | collective-permute-start | bytes 2359304 | tf_op jit(solution)/shard_map/ppermute | solution.py:29
  44.9 0.0 collective-permute-done.4.refs_1_.refs_3_
  44.9 17.1 %collective-permute-start.10 = (bf16[128,1536]{1,0:T(8,128)(2,1)}, bf16[128,1536]{1,0:T(8,128)(2,1)}, u32[]{:S(2)}, u32[]{:S(2)}) collective-permute-start(bf16[128,1536]{1,0:T(8,128)(2,1)} %collective-permute-done.1.refs_1_), channel_id=1, source_target_pairs={{0,1},{2,3},{4,5},{6,7},{8,9},{10,11},{12,13},{14,15},{1,0},{3,2},... | collective-permute-start | bytes 1179656 | tf_op jit(solution)/shard_map/ppermute | solution.py:29
  62.0 2.8 %shard_map.56 = bf16[128,3072]{1,0:T(8,128)(2,1)} custom-call(s32[6,16]{1,0:T(8,128)} %bitcast.17, bf16[512,1536]{1,0:T(8,128)(2,1)} %collective-permute-done.3.refs_0_.refs_2_, bf16[512,1536]{1,0:T(8,128)(2,1)} %collective-permute-done.4.refs_1_.refs_3_), custom_call_target="tpu_custom_call" | custom-call | bytes 1572864 | tf_op jit(solution)/shard_map/pallas_call | solution.py:90
  64.9 0.0 collective-permute-done.6.refs_0_.refs_1_
  64.9 1.9 %collective-permute-start.5 = (bf16[128,3072]{1,0:T(8,128)(2,1)}, bf16[128,3072]{1,0:T(8,128)(2,1)}, u32[]{:S(2)}, u32[]{:S(2)}) collective-permute-start(bf16[128,3072]{1,0:T(8,128)(2,1)} %shard_map.56), channel_id=1, source_target_pairs={{1,2},{3,4},{5,6},{7,8},{9,10},{11,12},{13,14},{2,1},{4,3},{6,5},{... | collective-permute-start | bytes 2359304 | tf_op jit(solution)/shard_map/ppermute | solution.py:29
  66.8 0.0 collective-permute-done.7.refs_2_.refs_3_
  66.8 1.5 %collective-permute-start.11 = (bf16[384,768]{1,0:T(8,128)(2,1)}, bf16[384,768]{1,0:T(8,128)(2,1)}, u32[]{:S(2)}, u32[]{:S(2)}) collective-permute-start(bf16[384,768]{1,0:T(8,128)(2,1)} %get-tuple-element.24), channel_id=1, source_target_pairs={{1,2},{5,6},{9,10},{13,14},{2,1},{6,5},{10,9},{14,13},{17,18},{21,... | collective-permute-start | bytes 1769480 | tf_op jit(solution)/shard_map/ppermute | solution.py:29
  68.3 0.0 collective-permute-done.refs_0_
  68.3 1.3 collective-permute-start.13
  69.6 2.5 %shard_map.57 = bf16[128,1536]{1,0:T(8,128)(2,1)} custom-call(s32[6,16]{1,0:T(8,128)} %bitcast.18, bf16[512,1536]{1,0:T(8,128)(2,1)} %collective-permute-done.refs_0_), custom_call_target="tpu_custom_call" | custom-call | bytes 786432 | tf_op jit(solution)/shard_map/pallas_call | solution.py:90
  72.1 0.0 collective-permute-done.8.refs_4_.refs_5_
  72.1 24.4 %collective-permute-start.9 = (bf16[128,1536]{1,0:T(8,128)(2,1)}, bf16[128,1536]{1,0:T(8,128)(2,1)}, u32[]{:S(2)}, u32[]{:S(2)}) collective-permute-start(bf16[128,1536]{1,0:T(8,128)(2,1)} %shard_map.57), channel_id=1, source_target_pairs={{0,1},{2,3},{4,5},{6,7},{8,9},{10,11},{12,13},{14,15},{1,0},{3,2},... | collective-permute-start | bytes 1179656 | tf_op jit(solution)/shard_map/ppermute | solution.py:29
  96.6 0.0 collective-permute-done.10.refs_7_
  96.6 5.6 %collective-permute-start.2 = (bf16[384,768]{1,0:T(8,128)(2,1)}, bf16[384,768]{1,0:T(8,128)(2,1)}, u32[]{:S(2)}, u32[]{:S(2)}) collective-permute-start(bf16[384,768]{1,0:T(8,128)(2,1)} %get-tuple-element.16), channel_id=1, source_target_pairs={{1,2},{3,4},{5,6},{7,8},{9,10},{11,12},{13,14},{2,1},{4,3},{6,5},{... | collective-permute-start | bytes 1769480 | tf_op jit(solution)/shard_map/ppermute | solution.py:29
  102.8 12.2 %shard_map.58 = (f32[1536,512]{1,0:T(8,128)}, f32[96,512]{1,0:T(8,128)}) custom-call(s32[1]{0:T(128)S(6)} %copy.12.window_ref, s32[6,16]{1,0:T(8,128)} %bitcast.19, bf16[512,1536]{1,0:T(8,128)(2,1)} %bitcast.5, bf16[512,1536]{1,0:T(8,128)(2,1)} %bitcast.12, bf16[512,1536]{1,0:T(8,128)(2,1)} %bitcast.15, ...), custom_call_target="tpu_custom_call" | custom-call | flops 3221225472 | bytes 9437184 | tf_op jit(solution)/shard_map/pallas_call | solution.py:249
  115.0 0.0 collective-permute-done.9.refs_6_
  115.0 9.0 %shard_map.59 = (f32[1536,512]{1,0:T(8,128)}, f32[96,512]{1,0:T(8,128)}) custom-call(s32[1]{0:T(128)S(6)} %copy.12.window_ref, s32[6,16]{1,0:T(8,128)} %bitcast.20, bf16[512,1536]{1,0:T(8,128)(2,1)} %bitcast.6, bf16[128,3072]{1,0:T(8,128)(2,1)} %collective-permute-done.6.refs_0_.refs_1_, ...), custom_call_target="tpu_custom_call", output_to_operand_aliasing={{0}: (11, {}), {1}: (12, {})} | custom-call | flops 1610612736 | bytes 9437184 | tf_op jit(solution)/shard_map/pallas_call | solution.py:249
  124.0 0.0 collective-permute-done.11.refs_2_
  124.1 0.0 collective-permute-done.13.refs_3_
  124.1 0.0 collective-permute-done.5.refs_4_.refs_5_.refs_3_
  124.1 6.4 %shard_map.60.refs_7_ = bf16[512,1536]{1,0:T(8,128)(2,1)} custom-call(s32[1]{0:T(128)S(6)} %copy.12.window_ref, s32[6,16]{1,0:T(8,128)} %bitcast.21, bf16[512,1536]{1,0:T(8,128)(2,1)} %bitcast.7, bf16[512,1536]{1,0:T(8,128)(2,1)} %collective-permute-done.refs_0_, bf16[128,1536]{1,0:T(8,128)(2,1)} %collective-permute-done.1.refs_1_, ...), custom_call_target="tpu_custom_call" | custom-call | flops 1006632960 | bytes 5111808 | tf_op jit(solution)/shard_map/pallas_call | solution.py:249
  130.5 0.0 collective-permute-done.2.refs_2_
  130.5 6.4 %shard_map.61 = bf16[512,1536]{1,0:T(8,128)(2,1)} custom-call(s32[1]{0:T(128)S(6)} %copy.12.window_ref, s32[6,16]{1,0:T(8,128)} %bitcast.22, bf16[512,1536]{1,0:T(8,128)(2,1)} %bitcast.8, bf16[512,1536]{1,0:T(8,128)(2,1)} %collective-permute-done.refs_0_, bf16[128,1536]{1,0:T(8,128)(2,1)} %collective-permute-done.1.refs_1_, ...), custom_call_target="tpu_custom_call", output_to_operand_aliasing={{}: (10, {})} | custom-call | flops 1006632960 | bytes 5111808 | tf_op jit(solution)/shard_map/pallas_call | solution.py:249
Async XLA Ops:
  0.0 41.9 %collective-permute-start.3 = (bf16[512,1536]{1,0:T(8,128)(2,1)}, bf16[512,1536]{1,0:T(8,128)(2,1)}, u32[]{:S(2)}, u32[]{:S(2)}) collective-permute-start(bf16[512,1536]{1,0:T(8,128)(2,1)} %bitcast.9), channel_id=1, source_target_pairs={{0,1},{2,3},{4,5},{6,7},{8,9},{10,11},{12,13},{14,15},{1,0},{3,2},... | collective-permute-start | bytes 4718600 | tf_op jit(solution)/shard_map/ppermute | solution.py:29
  0.7 44.2 %collective-permute-start.4 = (bf16[512,1536]{1,0:T(8,128)(2,1)}, bf16[512,1536]{1,0:T(8,128)(2,1)}, u32[]{:S(2)}, u32[]{:S(2)}) collective-permute-start(bf16[512,1536]{1,0:T(8,128)(2,1)} %bitcast.13), channel_id=1, source_target_pairs={{0,1},{2,3},{4,5},{6,7},{8,9},{10,11},{12,13},{14,15},{1,0},{3,2},... | collective-permute-start | bytes 4718600 | tf_op jit(solution)/shard_map/ppermute | solution.py:29
  0.7 67.6 %collective-permute-start = (bf16[512,1536]{1,0:T(8,128)(2,1)}, bf16[512,1536]{1,0:T(8,128)(2,1)}, u32[]{:S(2)}, u32[]{:S(2)}) collective-permute-start(bf16[512,1536]{1,0:T(8,128)(2,1)} %bitcast.10), channel_id=1, source_target_pairs={{1,2},{3,4},{5,6},{7,8},{9,10},{11,12},{13,14},{2,1},{4,3},{6,5},{... | collective-permute-start | bytes 4718600 | tf_op jit(solution)/shard_map/ppermute | solution.py:29
  9.1 29.6 %collective-permute-start.12 = (bf16[384,768]{1,0:T(8,128)(2,1)}, bf16[384,768]{1,0:T(8,128)(2,1)}, u32[]{:S(2)}, u32[]{:S(2)}) collective-permute-start(bf16[384,768]{1,0:T(8,128)(2,1)} %get-tuple-element.24), channel_id=1, source_target_pairs={{3,1},{7,5},{11,9},{4,6},{8,10},{12,14},{19,17},{23,21},{27,25},{2... | collective-permute-start | bytes 1769480 | tf_op jit(solution)/shard_map/ppermute | solution.py:29
  12.1 15.8 %collective-permute-start.1 = (bf16[128,1536]{1,0:T(8,128)(2,1)}, bf16[128,1536]{1,0:T(8,128)(2,1)}, u32[]{:S(2)}, u32[]{:S(2)}) collective-permute-start(bf16[128,1536]{1,0:T(8,128)(2,1)} %get-tuple-element.15), channel_id=1, source_target_pairs={{1,2},{3,4},{5,6},{7,8},{9,10},{11,12},{13,14},{2,1},{4,3},{6,5},{... | collective-permute-start | bytes 1179656 | tf_op jit(solution)/shard_map/ppermute | solution.py:29
  27.9 36.9 %collective-permute-start.6 = (bf16[128,3072]{1,0:T(8,128)(2,1)}, bf16[128,3072]{1,0:T(8,128)(2,1)}, u32[]{:S(2)}, u32[]{:S(2)}) collective-permute-start(bf16[128,3072]{1,0:T(8,128)(2,1)} %get-tuple-element.17), channel_id=1, source_target_pairs={{0,8},{1,9},{2,10},{3,11},{4,12},{5,13},{6,14},{7,15},{8,0},{9,1},... | collective-permute-start | bytes 2359304 | tf_op jit(solution)/shard_map/ppermute | solution.py:29
  38.7 28.1 %collective-permute-start.7 = (bf16[128,3072]{1,0:T(8,128)(2,1)}, bf16[128,3072]{1,0:T(8,128)(2,1)}, u32[]{:S(2)}, u32[]{:S(2)}) collective-permute-start(bf16[128,3072]{1,0:T(8,128)(2,1)} %get-tuple-element.18), channel_id=1, source_target_pairs={{0,4},{1,5},{2,6},{3,7},{4,8},{5,9},{6,10},{7,11},{8,12},{9,13},{1... | collective-permute-start | bytes 2359304 | tf_op jit(solution)/shard_map/ppermute | solution.py:29
  41.9 30.2 %collective-permute-start.8 = (bf16[128,3072]{1,0:T(8,128)(2,1)}, bf16[128,3072]{1,0:T(8,128)(2,1)}, u32[]{:S(2)}, u32[]{:S(2)}) collective-permute-start(bf16[128,3072]{1,0:T(8,128)(2,1)} %get-tuple-element.19), channel_id=1, source_target_pairs={{4,0},{5,1},{6,2},{7,3},{8,4},{9,5},{10,6},{11,7},{12,8},{13,9},{1... | collective-permute-start | bytes 2359304 | tf_op jit(solution)/shard_map/ppermute | solution.py:29
  44.9 51.7 %collective-permute-start.10 = (bf16[128,1536]{1,0:T(8,128)(2,1)}, bf16[128,1536]{1,0:T(8,128)(2,1)}, u32[]{:S(2)}, u32[]{:S(2)}) collective-permute-start(bf16[128,1536]{1,0:T(8,128)(2,1)} %collective-permute-done.1.refs_1_), channel_id=1, source_target_pairs={{0,1},{2,3},{4,5},{6,7},{8,9},{10,11},{12,13},{14,15},{1,0},{3,2},... | collective-permute-start | bytes 1179656 | tf_op jit(solution)/shard_map/ppermute | solution.py:29
  64.9 59.2 %collective-permute-start.5 = (bf16[128,3072]{1,0:T(8,128)(2,1)}, bf16[128,3072]{1,0:T(8,128)(2,1)}, u32[]{:S(2)}, u32[]{:S(2)}) collective-permute-start(bf16[128,3072]{1,0:T(8,128)(2,1)} %shard_map.56), channel_id=1, source_target_pairs={{1,2},{3,4},{5,6},{7,8},{9,10},{11,12},{13,14},{2,1},{4,3},{6,5},{... | collective-permute-start | bytes 2359304 | tf_op jit(solution)/shard_map/ppermute | solution.py:29
  66.8 57.2 %collective-permute-start.11 = (bf16[384,768]{1,0:T(8,128)(2,1)}, bf16[384,768]{1,0:T(8,128)(2,1)}, u32[]{:S(2)}, u32[]{:S(2)}) collective-permute-start(bf16[384,768]{1,0:T(8,128)(2,1)} %get-tuple-element.24), channel_id=1, source_target_pairs={{1,2},{5,6},{9,10},{13,14},{2,1},{6,5},{10,9},{14,13},{17,18},{21,... | collective-permute-start | bytes 1769480 | tf_op jit(solution)/shard_map/ppermute | solution.py:29
  68.3 55.7 %collective-permute-start.13 = (bf16[384,768]{1,0:T(8,128)(2,1)}, bf16[384,768]{1,0:T(8,128)(2,1)}, u32[]{:S(2)}, u32[]{:S(2)}) collective-permute-start(bf16[384,768]{1,0:T(8,128)(2,1)} %collective-permute-done.12), channel_id=1, source_target_pairs={{1,4},{5,8},{9,12},{6,3},{10,7},{14,11},{17,20},{21,24},{25,28},{2... | collective-permute-start | bytes 1769480 | tf_op jit(solution)/shard_map/ppermute | solution.py:29
  72.1 42.9 %collective-permute-start.9 = (bf16[128,1536]{1,0:T(8,128)(2,1)}, bf16[128,1536]{1,0:T(8,128)(2,1)}, u32[]{:S(2)}, u32[]{:S(2)}) collective-permute-start(bf16[128,1536]{1,0:T(8,128)(2,1)} %shard_map.57), channel_id=1, source_target_pairs={{0,1},{2,3},{4,5},{6,7},{8,9},{10,11},{12,13},{14,15},{1,0},{3,2},... | collective-permute-start | bytes 1179656 | tf_op jit(solution)/shard_map/ppermute | solution.py:29
  96.6 34.0 %collective-permute-start.2 = (bf16[384,768]{1,0:T(8,128)(2,1)}, bf16[384,768]{1,0:T(8,128)(2,1)}, u32[]{:S(2)}, u32[]{:S(2)}) collective-permute-start(bf16[384,768]{1,0:T(8,128)(2,1)} %get-tuple-element.16), channel_id=1, source_target_pairs={{1,2},{3,4},{5,6},{7,8},{9,10},{11,12},{13,14},{2,1},{4,3},{6,5},{... | collective-permute-start | bytes 1769480 | tf_op jit(solution)/shard_map/ppermute | solution.py:29

commit v5 on v4

--- a/solution.py
+++ b/solution.py
@@ -287,13 +287,27 @@
 
     outward = [(1, is_odd), (-1, is_even)]
     inward = [(1, is_even), (-1, is_odd)]
-    hop = [(-2, lambda f: f % 4 == 3 and f + 1 < frames), (2, lambda f: f % 4 == 0 and f > 0)]
-    skip = [(3, lambda f: f % 4 == 1), (-3, lambda f: f % 4 == 2)]
-
-    def turning(position):
-        return (position + 1) % 4 < 2
-
-    straight = [(1, lambda f: f % 4 == 1), (-1, lambda f: f % 4 == 2)]
+    middle = (frames // 4 - 1) // 2
+
+    def up(f, half):
+        return (f % 4 == 3) & (f + 1 < frames) & (f // 4 + half <= middle)
+
+    def down(f, half):
+        return (f % 4 == 0) & (f > 0) & (f // 4 - 1 - half >= middle)
+
+    def hop(half):
+        return [(-2, lambda f: up(f, half)), (2, lambda f: down(f, half))]
+
+    def skip(half):
+        return [(3, lambda f: up(f + 2, half)), (-3, lambda f: down(f - 2, half))]
+
+    def straight(half):
+        ahead = (1, lambda f: (f % 2 == 1) & (not up(f, half)))
+        return [ahead, (-1, lambda f: (f % 2 == 0) & (not down(f, half)))]
+
+    def turning(half):
+        return lambda position: up(position - 1, half) | down(position + 1, half)
+
     beyond_keys = moved(keys, outward)
     half = heads // 2
     halves = [(0, half), (half, heads - half)]
@@ -353,9 +367,10 @@
     around = []
     if shared:
         picked = moved(picked, outward)
-        around = [moved(lower, hop)]
-    lower = moved(lower, straight if shared else outward)
-    upper = moved(upper, outward)
+        around = [moved(lower, hop(0))]
+        around.append(moved(upper, hop(1)))
+    lower = moved(lower, straight(0) if shared else outward)
+    upper = moved(upper, straight(1) if shared else outward)
     arrived = []
     for block, (steps, _, _) in zip(blocks, far):
         arrived.append(moved(block, steps))
@@ -365,7 +380,8 @@
     if shared:
         (behind,) = gather(far_picks, [mate_keys, mate_values], [past], frames)
         behind = moved(behind, outward)
-        around = [moved(around[0], skip)]
+        lower_around = moved(around[0], skip(0))
+        upper_around = moved(around[1], skip(1))
 
     def always(position):
         return position >= 0
@@ -396,7 +412,7 @@
     distant.append((handed_keys, 0, [handed_values], [0], False, ahead_there, None))
     state = attend(win_rows, far_picks, query, distant, state, False)
     out = None
-    for part, values in ((halves[0], [lower, *around]), (halves[1], [upper])):
+    for which, part, values in ((0, halves[0], [lower, lower_around]), (1, halves[1], [upper, upper_around])):
         start = part[0]
         nearby = [
             (
@@ -406,7 +422,7 @@
                 [start] + [0] * len(values),
                 True,
                 near_there,
-                (partner, turning),
+                (partner, turning(which)),
             ),
             (behind, start, [behind], [heads + start], False, two_back, None),
         ]

time: 138 us -> 149 us (1.080)
  the two profiles are of different devices: /device:TPU:15 before, /device:TPU:1 now
where the time goes in v5:
time: 149 us
  waiting for transfers between devices  62 us (42%)
  Pallas kernels  44.3 us (30%)
  starting transfers between devices  41.5 us (28%)
    ppermute x16, waiting for transfers between devices, moved(): return lax.ppermute(value, 'frame', pairs)  62 us
    ppermute x16, starting transfers between devices, moved(): return lax.ppermute(value, 'frame', pairs)  41.5 us
    pallas_call x4, Pallas kernels, attend(): pl.pallas_call(functools.partial(attend_kernel, kinds, together, state is...  34.1 us
    pallas_call x3, Pallas kernels, gather(): pl.pallas_call(functools.partial(gather_kernel, readers, frames, len(arra...  10.2 us
  transfers between devices with their start and end apart: 16, of which 4 were waited for; matrix products, arithmetic and copies ran while one was open for 0% of the time, Pallas kernels for 25%

profile of v5, /device:TPU:1, one launch (start us, length us, event | category | flops | bytes accessed | tf_op | source)
XLA Modules:
  0.0 148.7 jit_solution(5094330704117503651)
XLA Ops:
  0.0 4.5 %collective-permute-start = (bf16[512,1536]{1,0:T(8,128)(2,1)}, bf16[512,1536]{1,0:T(8,128)(2,1)}, u32[]{:S(2)}, u32[]{:S(2)}) collective-permute-start(bf16[512,1536]{1,0:T(8,128)(2,1)} %bitcast.9), channel_id=1, source_target_pairs={{1,2},{3,4},{5,6},{7,8},{9,10},{11,12},{13,14},{2,1},{4,3},{6,5},{... | collective-permute-start | bytes 4718600 | tf_op jit(solution)/shard_map/ppermute | solution.py:29
  4.5 0.1 collective-permute-start.5
  4.6 0.5 collective-permute-start.6
  5.1 4.9 %shard_map.55 = (bf16[128,3072]{1,0:T(8,128)(2,1)}, bf16[128,3072]{1,0:T(8,128)(2,1)}, bf16[128,3072]{1,0:T(8,128)(2,1)}, bf16[128,1536]{1,0:T(8,128)(2,1)}, bf1...) custom-call(s32[6,16]{1,0:T(8,128)} %bitcast.16, bf16[512,1536]{1,0:T(8,128)(2,1)} %bitcast.11, bf16[512,1536]{1,0:T(8,128)(2,1)} %bitcast.14), custom_call_target="tpu_custom_call" | custom-call | bytes 7864320 | tf_op jit(solution)/shard_map/pallas_call | solution.py:90
  10.0 3.1 %collective-permute-start.1 = (bf16[128,1536]{1,0:T(8,128)(2,1)}, bf16[128,1536]{1,0:T(8,128)(2,1)}, u32[]{:S(2)}, u32[]{:S(2)}) collective-permute-start(bf16[128,1536]{1,0:T(8,128)(2,1)} %get-tuple-element.15), channel_id=1, source_target_pairs={{1,2},{3,4},{5,6},{7,8},{9,10},{11,12},{13,14},{2,1},{4,3},{6,5},{... | collective-permute-start | bytes 1179656 | tf_op jit(solution)/shard_map/ppermute | solution.py:29
  13.2 1.3 collective-permute-start.3
  14.5 33.0 %collective-permute-done.1.refs_1_ = bf16[128,1536]{1,0:T(8,128)(2,1)} collective-permute-done((bf16[128,1536]{1,0:T(8,128)(2,1)}, bf16[128,1536]{1,0:T(8,128)(2,1)}, u32[]{:S(2)}, u32[]{:S(2)}) %collective-permute-start.1) | collective-permute-done | bytes 393248 | tf_op jit(solution)/shard_map/ppermute | solution.py:29
  47.5 1.3 collective-permute-start.14
  48.7 0.0 collective-permute-done.3
  48.8 3.3 %collective-permute-start.8 = (bf16[128,3072]{1,0:T(8,128)(2,1)}, bf16[128,3072]{1,0:T(8,128)(2,1)}, u32[]{:S(2)}, u32[]{:S(2)}) collective-permute-start(bf16[128,3072]{1,0:T(8,128)(2,1)} %get-tuple-element.17), channel_id=1, source_target_pairs={{0,8},{1,9},{2,10},{3,11},{4,12},{5,13},{6,14},{7,15},{8,0},{9,1},... | collective-permute-start | bytes 2359304 | tf_op jit(solution)/shard_map/ppermute | solution.py:29
  52.0 6.4 %collective-permute-done.14 = bf16[384,768]{1,0:T(8,128)(2,1)} collective-permute-done((bf16[384,768]{1,0:T(8,128)(2,1)}, bf16[384,768]{1,0:T(8,128)(2,1)}, u32[]{:S(2)}, u32[]{:S(2)}) %collective-permute-start.14) | collective-permute-done | bytes 589856 | tf_op jit(solution)/shard_map/ppermute | solution.py:29
  58.4 5.1 %collective-permute-start.9 = (bf16[128,3072]{1,0:T(8,128)(2,1)}, bf16[128,3072]{1,0:T(8,128)(2,1)}, u32[]{:S(2)}, u32[]{:S(2)}) collective-permute-start(bf16[128,3072]{1,0:T(8,128)(2,1)} %get-tuple-element.18), channel_id=1, source_target_pairs={{0,4},{1,5},{2,6},{3,7},{4,8},{5,9},{6,10},{7,11},{8,12},{9,13},{1... | collective-permute-start | bytes 2359304 | tf_op jit(solution)/shard_map/ppermute | solution.py:29
  63.5 0.0 collective-permute-done.refs_0_
  63.5 1.3 collective-permute-start.10
  64.8 2.5 %shard_map.57 = bf16[128,1536]{1,0:T(8,128)(2,1)} custom-call(s32[6,16]{1,0:T(8,128)} %bitcast.17, bf16[512,1536]{1,0:T(8,128)(2,1)} %collective-permute-done.refs_0_), custom_call_target="tpu_custom_call" | custom-call | bytes 786432 | tf_op jit(solution)/shard_map/pallas_call | solution.py:90
  67.3 0.0 collective-permute-done.5.refs_0_.refs_2_
  67.3 0.1 collective-permute-start.12
  67.4 0.0 collective-permute-done.6.refs_1_.refs_3_
  67.4 0.5 collective-permute-start.11
  67.9 2.8 %shard_map.56 = bf16[128,3072]{1,0:T(8,128)(2,1)} custom-call(s32[6,16]{1,0:T(8,128)} %bitcast.18, bf16[512,1536]{1,0:T(8,128)(2,1)} %collective-permute-done.5.refs_0_.refs_2_, bf16[512,1536]{1,0:T(8,128)(2,1)} %collective-permute-done.6.refs_1_.refs_3_), custom_call_target="tpu_custom_call" | custom-call | bytes 1572864 | tf_op jit(solution)/shard_map/pallas_call | solution.py:90
  70.7 15.5 %collective-permute-done.8.refs_0_.refs_1_ = bf16[128,3072]{1,0:T(8,128)(2,1)} collective-permute-done((bf16[128,3072]{1,0:T(8,128)(2,1)}, bf16[128,3072]{1,0:T(8,128)(2,1)}, u32[]{:S(2)}, u32[]{:S(2)}) %collective-permute-start.8) | collective-permute-done | bytes 786464 | tf_op jit(solution)/shard_map/ppermute | solution.py:29
  86.2 5.7 %collective-permute-start.7 = (bf16[128,3072]{1,0:T(8,128)(2,1)}, bf16[128,3072]{1,0:T(8,128)(2,1)}, u32[]{:S(2)}, u32[]{:S(2)}) collective-permute-start(bf16[128,3072]{1,0:T(8,128)(2,1)} %shard_map.56), channel_id=1, source_target_pairs={{1,2},{3,4},{5,6},{7,8},{9,10},{11,12},{13,14},{2,1},{4,3},{6,5},{... | collective-permute-start | bytes 2359304 | tf_op jit(solution)/shard_map/ppermute | solution.py:29
  91.9 0.0 collective-permute-done.9.refs_2_.refs_3_
  91.9 1.9 %collective-permute-start.13 = (bf16[384,768]{1,0:T(8,128)(2,1)}, bf16[384,768]{1,0:T(8,128)(2,1)}, u32[]{:S(2)}, u32[]{:S(2)}) collective-permute-start(bf16[384,768]{1,0:T(8,128)(2,1)} %get-tuple-element.24), channel_id=1, source_target_pairs={{1,2},{5,6},{9,10},{11,12},{13,14},{2,1},{4,3},{6,5},{10,9},{14,13... | collective-permute-start | bytes 1769480 | tf_op jit(solution)/shard_map/ppermute | solution.py:29
  93.8 7.1 %collective-permute-done.10.refs_4_.refs_5_ = bf16[128,3072]{1,0:T(8,128)(2,1)} collective-permute-done((bf16[128,3072]{1,0:T(8,128)(2,1)}, bf16[128,3072]{1,0:T(8,128)(2,1)}, u32[]{:S(2)}, u32[]{:S(2)}) %collective-permute-start.10) | collective-permute-done | bytes 786464 | tf_op jit(solution)/shard_map/ppermute | solution.py:29
  100.9 8.9 %collective-permute-start.15 = (bf16[384,768]{1,0:T(8,128)(2,1)}, bf16[384,768]{1,0:T(8,128)(2,1)}, u32[]{:S(2)}, u32[]{:S(2)}) collective-permute-start(bf16[384,768]{1,0:T(8,128)(2,1)} %collective-permute-done.14), channel_id=1, source_target_pairs={{1,4},{5,8},{10,7},{14,11},{17,20},{21,24},{26,23},{30,27}} | collective-permute-start | bytes 1769480 | tf_op jit(solution)/shard_map/ppermute | solution.py:29
  109.8 0.0 collective-permute-done.12.refs_7_
  109.8 1.9 %collective-permute-start.2 = (bf16[384,768]{1,0:T(8,128)(2,1)}, bf16[384,768]{1,0:T(8,128)(2,1)}, u32[]{:S(2)}, u32[]{:S(2)}) collective-permute-start(bf16[384,768]{1,0:T(8,128)(2,1)} %get-tuple-element.16), channel_id=1, source_target_pairs={{1,2},{5,6},{7,8},{9,10},{11,12},{13,14},{2,1},{4,3},{6,5},{8,7},{... | collective-permute-start | bytes 1769480 | tf_op jit(solution)/shard_map/ppermute | solution.py:29
  111.7 0.0 collective-permute-done.11.refs_6_
  111.7 2.1 %collective-permute-start.4 = (bf16[384,768]{1,0:T(8,128)(2,1)}, bf16[384,768]{1,0:T(8,128)(2,1)}, u32[]{:S(2)}, u32[]{:S(2)}) collective-permute-start(bf16[384,768]{1,0:T(8,128)(2,1)} %collective-permute-done.3), channel_id=1, source_target_pairs={{1,4},{14,11},{17,20},{30,27}} | collective-permute-start | bytes 1769480 | tf_op jit(solution)/shard_map/ppermute | solution.py:29
  114.5 12.2 %shard_map.58 = (f32[1536,512]{1,0:T(8,128)}, f32[96,512]{1,0:T(8,128)}) custom-call(s32[1]{0:T(128)S(6)} %copy.12.window_ref, s32[6,16]{1,0:T(8,128)} %bitcast.19, bf16[512,1536]{1,0:T(8,128)(2,1)} %bitcast.5, bf16[512,1536]{1,0:T(8,128)(2,1)} %bitcast.12, bf16[512,1536]{1,0:T(8,128)(2,1)} %bitcast.15, ...), custom_call_target="tpu_custom_call" | custom-call | flops 3221225472 | bytes 9437184 | tf_op jit(solution)/shard_map/pallas_call | solution.py:249
  126.7 9.0 %shard_map.59 = (f32[1536,512]{1,0:T(8,128)}, f32[96,512]{1,0:T(8,128)}) custom-call(s32[1]{0:T(128)S(6)} %copy.12.window_ref, s32[6,16]{1,0:T(8,128)} %bitcast.20, bf16[512,1536]{1,0:T(8,128)(2,1)} %bitcast.6, bf16[128,3072]{1,0:T(8,128)(2,1)} %collective-permute-done.8.refs_0_.refs_1_, ...), custom_call_target="tpu_custom_call", output_to_operand_aliasing={{0}: (11, {}), {1}: (12, {})} | custom-call | flops 1610612736 | bytes 9437184 | tf_op jit(solution)/shard_map/pallas_call | solution.py:249
  135.7 0.0 collective-permute-done.13.refs_2_
  135.7 0.0 collective-permute-done.15.refs_3_
  135.7 0.0 collective-permute-done.7.refs_4_.refs_5_
  135.7 6.4 %shard_map.60.refs_8_ = bf16[512,1536]{1,0:T(8,128)(2,1)} custom-call(s32[1]{0:T(128)S(6)} %copy.12.window_ref, s32[6,16]{1,0:T(8,128)} %bitcast.21, bf16[512,1536]{1,0:T(8,128)(2,1)} %bitcast.7, bf16[512,1536]{1,0:T(8,128)(2,1)} %collective-permute-done.refs_0_, bf16[128,1536]{1,0:T(8,128)(2,1)} %collective-permute-done.1.refs_1_, ...), custom_call_target="tpu_custom_call" | custom-call | flops 1006632960 | bytes 5111808 | tf_op jit(solution)/shard_map/pallas_call | solution.py:249
  142.2 0.0 collective-permute-done.2.refs_2_
  142.2 0.0 collective-permute-done.4.refs_3_
  142.2 6.5 %shard_map.61 = bf16[512,1536]{1,0:T(8,128)(2,1)} custom-call(s32[1]{0:T(128)S(6)} %copy.12.window_ref, s32[6,16]{1,0:T(8,128)} %bitcast.22, bf16[512,1536]{1,0:T(8,128)(2,1)} %bitcast.8, bf16[512,1536]{1,0:T(8,128)(2,1)} %collective-permute-done.refs_0_, bf16[128,1536]{1,0:T(8,128)(2,1)} %collective-permute-done.1.refs_1_, ...), custom_call_target="tpu_custom_call", output_to_operand_aliasing={{}: (11, {})} | custom-call | flops 1006632960 | bytes 5111808 | tf_op jit(solution)/shard_map/pallas_call | solution.py:249
Async XLA Ops:
  0.0 63.5 %collective-permute-start = (bf16[512,1536]{1,0:T(8,128)(2,1)}, bf16[512,1536]{1,0:T(8,128)(2,1)}, u32[]{:S(2)}, u32[]{:S(2)}) collective-permute-start(bf16[512,1536]{1,0:T(8,128)(2,1)} %bitcast.9), channel_id=1, source_target_pairs={{1,2},{3,4},{5,6},{7,8},{9,10},{11,12},{13,14},{2,1},{4,3},{6,5},{... | collective-permute-start | bytes 4718600 | tf_op jit(solution)/shard_map/ppermute | solution.py:29
  4.5 62.8 %collective-permute-start.5 = (bf16[512,1536]{1,0:T(8,128)(2,1)}, bf16[512,1536]{1,0:T(8,128)(2,1)}, u32[]{:S(2)}, u32[]{:S(2)}) collective-permute-start(bf16[512,1536]{1,0:T(8,128)(2,1)} %bitcast.10), channel_id=1, source_target_pairs={{0,1},{2,3},{4,5},{6,7},{8,9},{10,11},{12,13},{14,15},{1,0},{3,2},... | collective-permute-start | bytes 4718600 | tf_op jit(solution)/shard_map/ppermute | solution.py:29
  4.6 62.8 %collective-permute-start.6 = (bf16[512,1536]{1,0:T(8,128)(2,1)}, bf16[512,1536]{1,0:T(8,128)(2,1)}, u32[]{:S(2)}, u32[]{:S(2)}) collective-permute-start(bf16[512,1536]{1,0:T(8,128)(2,1)} %bitcast.13), channel_id=1, source_target_pairs={{0,1},{2,3},{4,5},{6,7},{8,9},{10,11},{12,13},{14,15},{1,0},{3,2},... | collective-permute-start | bytes 4718600 | tf_op jit(solution)/shard_map/ppermute | solution.py:29
  10.0 37.4 %collective-permute-start.1 = (bf16[128,1536]{1,0:T(8,128)(2,1)}, bf16[128,1536]{1,0:T(8,128)(2,1)}, u32[]{:S(2)}, u32[]{:S(2)}) collective-permute-start(bf16[128,1536]{1,0:T(8,128)(2,1)} %get-tuple-element.15), channel_id=1, source_target_pairs={{1,2},{3,4},{5,6},{7,8},{9,10},{11,12},{13,14},{2,1},{4,3},{6,5},{... | collective-permute-start | bytes 1179656 | tf_op jit(solution)/shard_map/ppermute | solution.py:29
  13.2 35.6 %collective-permute-start.3 = (bf16[384,768]{1,0:T(8,128)(2,1)}, bf16[384,768]{1,0:T(8,128)(2,1)}, u32[]{:S(2)}, u32[]{:S(2)}) collective-permute-start(bf16[384,768]{1,0:T(8,128)(2,1)} %get-tuple-element.16), channel_id=1, source_target_pairs={{3,1},{12,14},{19,17},{28,30}} | collective-permute-start | bytes 1769480 | tf_op jit(solution)/shard_map/ppermute | solution.py:29
  47.5 10.9 %collective-permute-start.14 = (bf16[384,768]{1,0:T(8,128)(2,1)}, bf16[384,768]{1,0:T(8,128)(2,1)}, u32[]{:S(2)}, u32[]{:S(2)}) collective-permute-start(bf16[384,768]{1,0:T(8,128)(2,1)} %get-tuple-element.24), channel_id=1, source_target_pairs={{3,1},{7,5},{8,10},{12,14},{19,17},{23,21},{24,26},{28,30}} | collective-permute-start | bytes 1769480 | tf_op jit(solution)/shard_map/ppermute | solution.py:29
  48.8 37.5 %collective-permute-start.8 = (bf16[128,3072]{1,0:T(8,128)(2,1)}, bf16[128,3072]{1,0:T(8,128)(2,1)}, u32[]{:S(2)}, u32[]{:S(2)}) collective-permute-start(bf16[128,3072]{1,0:T(8,128)(2,1)} %get-tuple-element.17), channel_id=1, source_target_pairs={{0,8},{1,9},{2,10},{3,11},{4,12},{5,13},{6,14},{7,15},{8,0},{9,1},... | collective-permute-start | bytes 2359304 | tf_op jit(solution)/shard_map/ppermute | solution.py:29
  58.4 33.5 %collective-permute-start.9 = (bf16[128,3072]{1,0:T(8,128)(2,1)}, bf16[128,3072]{1,0:T(8,128)(2,1)}, u32[]{:S(2)}, u32[]{:S(2)}) collective-permute-start(bf16[128,3072]{1,0:T(8,128)(2,1)} %get-tuple-element.18), channel_id=1, source_target_pairs={{0,4},{1,5},{2,6},{3,7},{4,8},{5,9},{6,10},{7,11},{8,12},{9,13},{1... | collective-permute-start | bytes 2359304 | tf_op jit(solution)/shard_map/ppermute | solution.py:29
  63.5 37.4 %collective-permute-start.10 = (bf16[128,3072]{1,0:T(8,128)(2,1)}, bf16[128,3072]{1,0:T(8,128)(2,1)}, u32[]{:S(2)}, u32[]{:S(2)}) collective-permute-start(bf16[128,3072]{1,0:T(8,128)(2,1)} %get-tuple-element.19), channel_id=1, source_target_pairs={{4,0},{5,1},{6,2},{7,3},{8,4},{9,5},{10,6},{11,7},{12,8},{13,9},{1... | collective-permute-start | bytes 2359304 | tf_op jit(solution)/shard_map/ppermute | solution.py:29
  67.3 42.4 %collective-permute-start.12 = (bf16[128,1536]{1,0:T(8,128)(2,1)}, bf16[128,1536]{1,0:T(8,128)(2,1)}, u32[]{:S(2)}, u32[]{:S(2)}) collective-permute-start(bf16[128,1536]{1,0:T(8,128)(2,1)} %collective-permute-done.1.refs_1_), channel_id=1, source_target_pairs={{0,1},{2,3},{4,5},{6,7},{8,9},{10,11},{12,13},{14,15},{1,0},{3,2},... | collective-permute-start | bytes 1179656 | tf_op jit(solution)/shard_map/ppermute | solution.py:29
  67.4 44.3 %collective-permute-start.11 = (bf16[128,1536]{1,0:T(8,128)(2,1)}, bf16[128,1536]{1,0:T(8,128)(2,1)}, u32[]{:S(2)}, u32[]{:S(2)}) collective-permute-start(bf16[128,1536]{1,0:T(8,128)(2,1)} %shard_map.57), channel_id=1, source_target_pairs={{0,1},{2,3},{4,5},{6,7},{8,9},{10,11},{12,13},{14,15},{1,0},{3,2},... | collective-permute-start | bytes 1179656 | tf_op jit(solution)/shard_map/ppermute | solution.py:29
  86.2 49.5 %collective-permute-start.7 = (bf16[128,3072]{1,0:T(8,128)(2,1)}, bf16[128,3072]{1,0:T(8,128)(2,1)}, u32[]{:S(2)}, u32[]{:S(2)}) collective-permute-start(bf16[128,3072]{1,0:T(8,128)(2,1)} %shard_map.56), channel_id=1, source_target_pairs={{1,2},{3,4},{5,6},{7,8},{9,10},{11,12},{13,14},{2,1},{4,3},{6,5},{... | collective-permute-start | bytes 2359304 | tf_op jit(solution)/shard_map/ppermute | solution.py:29
  91.9 43.8 %collective-permute-start.13 = (bf16[384,768]{1,0:T(8,128)(2,1)}, bf16[384,768]{1,0:T(8,128)(2,1)}, u32[]{:S(2)}, u32[]{:S(2)}) collective-permute-start(bf16[384,768]{1,0:T(8,128)(2,1)} %get-tuple-element.24), channel_id=1, source_target_pairs={{1,2},{5,6},{9,10},{11,12},{13,14},{2,1},{4,3},{6,5},{10,9},{14,13... | collective-permute-start | bytes 1769480 | tf_op jit(solution)/shard_map/ppermute | solution.py:29
  100.9 34.8 %collective-permute-start.15 = (bf16[384,768]{1,0:T(8,128)(2,1)}, bf16[384,768]{1,0:T(8,128)(2,1)}, u32[]{:S(2)}, u32[]{:S(2)}) collective-permute-start(bf16[384,768]{1,0:T(8,128)(2,1)} %collective-permute-done.14), channel_id=1, source_target_pairs={{1,4},{5,8},{10,7},{14,11},{17,20},{21,24},{26,23},{30,27}} | collective-permute-start | bytes 1769480 | tf_op jit(solution)/shard_map/ppermute | solution.py:29
  109.8 32.4 %collective-permute-start.2 = (bf16[384,768]{1,0:T(8,128)(2,1)}, bf16[384,768]{1,0:T(8,128)(2,1)}, u32[]{:S(2)}, u32[]{:S(2)}) collective-permute-start(bf16[384,768]{1,0:T(8,128)(2,1)} %get-tuple-element.16), channel_id=1, source_target_pairs={{1,2},{5,6},{7,8},{9,10},{11,12},{13,14},{2,1},{4,3},{6,5},{8,7},{... | collective-permute-start | bytes 1769480 | tf_op jit(solution)/shard_map/ppermute | solution.py:29
  111.7 30.5 %collective-permute-start.4 = (bf16[384,768]{1,0:T(8,128)(2,1)}, bf16[384,768]{1,0:T(8,128)(2,1)}, u32[]{:S(2)}, u32[]{:S(2)}) collective-permute-start(bf16[384,768]{1,0:T(8,128)(2,1)} %collective-permute-done.3), channel_id=1, source_target_pairs={{1,4},{14,11},{17,20},{30,27}} | collective-permute-start | bytes 1769480 | tf_op jit(solution)/shard_map/ppermute | solution.py:29
